TPU v7x, 128 devices: a whole 4x4x4 slice. The times are simulated.
128 devices in a mesh: seq: 32 (over y, z, core), wide: 4 (over x).
Axes of the slice: x: 4, y: 4, z: 4, core: 2. Of those that a mesh axis runs over, the one named last changes fastest.
Arguments:
- tokens: bfloat16 [49152, 1024], P('seq'), may hold values from -81 to 81
- shared_weight: bfloat16 [1024, 1024], P(None, 'wide'), may hold values from -0.1875 to 0.1875
- value_weight: bfloat16 [1024, 1024], P(None, 'wide'), may hold values from -0.1875 to 0.1875
- output_weight: bfloat16 [1024, 1024], P('wide'), may hold values from -0.1875 to 0.1875
- cotangent: bfloat16 [49152, 1024], P('seq'), may hold values from -6 to 6
- block_clusters: int32 [4, 384], P('wide', 'seq'), may hold values from 0 to 255, as said below
Outputs:
- token_grads: bfloat16 [49152, 1024], P('seq', 'wide')
- shared_grads: float32 [1024, 1024], P('seq', 'wide')
- value_grads: float32 [1024, 1024], P('seq', 'wide')
- output_grads: float32 [1024, 1024], P('wide', 'seq')
Inputs may be any that keep to these rules, and one draw needn't show every extreme that they name: `block_clusters`: group o holds clusters o * 8 to (o + 1) * 8 - 1. For each routed head: the blocks of one device along seq have at most 2 blocks in the clusters of any one group; some group receives exactly 2 blocks from every device, and each of its clusters then holds 8 blocks; no cluster holds more than 8 blocks.
All inputs are finite; a program needn't handle non-finite values.
Results may differ from a plain program's by a relative error of at most 0.012.
The roundings to bfloat16 on the way count: a program that leaves them out, or rounds other values in their place, can miss the bound.
Values may be sent and summed in bfloat16 or wider, within the bound.
A program may use at most 128 MiB of HBM per device.

v0:
```python
import math

import jax
import jax.numpy as jnp
from jax import lax
from jax.sharding import PartitionSpec as P

HEAD = 128
WINDOW = 256
BLOCK = 128
CLUS_DEV = 8


EPSILON = 1e-06
NEGATIVE = -1e30


def shifted(value, axis, steps):
    count = lax.axis_size(axis)
    first, last = (max(0, -steps), min(count, count - steps))
    return lax.ppermute(value, axis, [(source, source + steps) for source in range(first, last)])


def contract(left_side, right_side, left_dim, right_dim):
    return lax.dot_general(
        left_side,
        right_side,
        (((left_dim,), (right_dim,)), ((), ())),
        preferred_element_type=jnp.float32,
    )


def unit_keys(queries):
    floats = queries.astype(jnp.float32)
    factor = lax.rsqrt(jnp.mean(floats * floats, axis=-1, keepdims=True) + EPSILON)
    return ((floats * factor).astype(jnp.bfloat16), factor)


def key_chain(queries, factor, key_grads):
    floats = queries.astype(jnp.float32)
    inner_sum = jnp.sum(floats * key_grads, axis=-1, keepdims=True)
    return factor * key_grads - factor**3 / floats.shape[-1] * floats * inner_sum


def attend(queries, key_rows, values, cotangent_rows, allowed, self_spot, want_grads):
    head_scale = 1.0 / math.sqrt(queries.shape[-1])
    scores = contract(queries, key_rows, 1, 1) * head_scale
    scores = jnp.where(self_spot, 0.0, scores)
    scores = jnp.where(allowed, scores, NEGATIVE)
    highest = jnp.max(scores, axis=1, keepdims=True)
    weights = jnp.where(allowed, jnp.exp(scores - highest), 0.0)
    probs_full = weights / jnp.sum(weights, axis=1, keepdims=True)
    probs_half = probs_full.astype(jnp.bfloat16)
    outputs = contract(probs_half, values, 1, 0).astype(jnp.bfloat16)
    if not want_grads:
        return outputs
    prob_grads = contract(cotangent_rows, values, 1, 1)
    centre = jnp.sum(probs_full * prob_grads, axis=1, keepdims=True)
    score_grads = jnp.where(self_spot, 0.0, probs_full * (prob_grads - centre))
    score_half = (score_grads * head_scale).astype(jnp.bfloat16)
    query_grads = contract(score_half, key_rows, 1, 0)
    key_grads = contract(score_half, queries, 0, 0)
    value_grads = contract(probs_half, cotangent_rows, 0, 0)
    return (outputs, query_grads, key_grads, value_grads)


def band_pass(query_ext, value_ext, tangent_ext, first_position, seq_tokens, window, tile_rows):
    length = query_ext.shape[0]
    feature_width = query_ext.shape[1]
    queries_count = length - window
    tile_total = -(-queries_count // tile_rows)
    padded = window + tile_total * tile_rows
    key_pad, factor = unit_keys(query_ext)
    rows_at = jnp.arange(padded, dtype=jnp.int32)
    positions = first_position + rows_at
    usable = (positions >= 0) & (positions < seq_tokens) & (rows_at < length)
    offsets = (
        window
        + jnp.arange(tile_rows, dtype=jnp.int32)[:, None]
        - jnp.arange(tile_rows + window, dtype=jnp.int32)[None, :]
    )
    in_band = (offsets >= 0) & (offsets <= window)
    self_spot = offsets == 0

    def visit_tile(tile_index, carried):
        key_sums, value_sums, out_rows, query_rows = carried
        tile_start = (tile_index * tile_rows).astype(jnp.int32)
        queries = lax.dynamic_slice_in_dim(query_ext, tile_start + window, tile_rows, 0)
        key_rows = lax.dynamic_slice_in_dim(key_pad, tile_start, tile_rows + window, 0)
        values = lax.dynamic_slice_in_dim(value_ext, tile_start, tile_rows + window, 0)
        tangents = lax.dynamic_slice_in_dim(tangent_ext, tile_start + window, tile_rows, 0)
        key_usable = lax.dynamic_slice_in_dim(usable, tile_start, tile_rows + window, 0)
        allowed = in_band & key_usable[None, :] | self_spot
        outputs, query_grads, key_grads, value_grads = attend(
            queries, key_rows, values, tangents, allowed, self_spot, True
        )
        old_keys = lax.dynamic_slice_in_dim(key_sums, tile_start, tile_rows + window, 0)
        key_sums = lax.dynamic_update_slice_in_dim(key_sums, old_keys + key_grads, tile_start, 0)
        old_values = lax.dynamic_slice_in_dim(value_sums, tile_start, tile_rows + window, 0)
        value_sums = lax.dynamic_update_slice_in_dim(
            value_sums, old_values + value_grads, tile_start, 0
        )
        out_rows = lax.dynamic_update_slice_in_dim(out_rows, outputs, tile_start, 0)
        query_rows = lax.dynamic_update_slice_in_dim(query_rows, query_grads, tile_start, 0)
        return (key_sums, value_sums, out_rows, query_rows)

    initial = (
        jnp.zeros((padded, feature_width), jnp.float32),
        jnp.zeros((padded, feature_width), jnp.float32),
        jnp.zeros((tile_total * tile_rows, feature_width), jnp.bfloat16),
        jnp.zeros((tile_total * tile_rows, feature_width), jnp.float32),
    )
    key_sums, value_sums, out_rows, query_rows = lax.fori_loop(0, tile_total, visit_tile, initial)
    return (out_rows, query_rows, key_sums, value_sums, factor)


def cluster_pass(packed, want_grads):
    row_count = packed.shape[0]
    queries = packed[:, :HEAD]
    values = packed[:, HEAD : 2 * HEAD]
    key_rows, factor = unit_keys(queries)
    row_order = jnp.arange(row_count, dtype=jnp.int32)
    allowed = row_order[None, :] <= row_order[:, None]
    self_spot = row_order[None, :] == row_order[:, None]
    if not want_grads:
        return attend(queries, key_rows, values, None, allowed, self_spot, False)
    tangents = packed[:, 2 * HEAD :]
    outputs, query_grads, key_grads, value_grads = attend(
        queries, key_rows, values, tangents, allowed, self_spot, True
    )
    query_total = (query_grads + key_chain(queries, factor, key_grads)).astype(jnp.bfloat16)
    return jnp.concatenate([outputs, query_total, value_grads.astype(jnp.bfloat16)], axis=1)


def full_pass(cluster_rows):
    return cluster_pass(cluster_rows, True)


def forward_pass(cluster_rows):
    return cluster_pass(cluster_rows, False)


def on_device(tokens, shared_weight, value_weight, output_weight, cotangent, block_clusters):
    seq_count = lax.axis_size("seq")
    position = lax.axis_index("seq")
    token_count = tokens.shape[0]
    seq_tokens = seq_count * token_count
    tile_rows = min(512, token_count)
    shared = contract(tokens, shared_weight, 1, 0).astype(jnp.bfloat16)
    valued = contract(tokens, value_weight, 1, 0).astype(jnp.bfloat16)
    head_cotangent = contract(cotangent, output_weight, 1, 1).astype(jnp.bfloat16)
    local_query = shared[:, :HEAD]
    local_value = valued[:, :HEAD]
    local_tangent = head_cotangent[:, :HEAD]
    routed_query = shared[:, HEAD:]
    routed_value = valued[:, HEAD:]
    routed_tangent = head_cotangent[:, HEAD:]
    first_position = position * token_count - WINDOW
    trailing = jnp.concatenate(
        [local_query[token_count - WINDOW :], local_value[token_count - WINDOW :]], axis=1
    )
    leading = shifted(trailing, "seq", 1)
    query_ext = jnp.concatenate([leading[:, :HEAD], local_query], axis=0)
    value_ext = jnp.concatenate([leading[:, HEAD:], local_value], axis=0)
    tangent_ext = jnp.concatenate([jnp.zeros((WINDOW, HEAD), jnp.bfloat16), local_tangent], axis=0)
    outputs, query_grads, key_all, value_all_rows, factor = band_pass(
        query_ext, value_ext, tangent_ext, first_position, seq_tokens, WINDOW, tile_rows
    )
    returned = shifted(
        jnp.concatenate([key_all[:WINDOW], value_all_rows[:WINDOW]], axis=1), "seq", -1
    )
    key_grads = jnp.concatenate(
        [key_all[WINDOW:token_count], key_all[token_count:] + returned[:, :HEAD]], axis=0
    )
    value_grads = jnp.concatenate(
        [value_all_rows[WINDOW:token_count], value_all_rows[token_count:] + returned[:, HEAD:]],
        axis=0,
    )
    factor = factor[WINDOW:]
    local_dq = (query_grads + key_chain(local_query, factor, key_grads)).astype(jnp.bfloat16)
    local_dv = value_grads.astype(jnp.bfloat16)
    block_count = token_count // BLOCK
    send_most = max(2, (block_count + seq_count - 1) // seq_count)
    slot_count = seq_count * send_most
    capacity = slot_count // CLUS_DEV
    labels = block_clusters[0]
    owners = labels // CLUS_DEV
    block_order = jnp.arange(block_count, dtype=jnp.int32)
    block_ranks = jnp.sum(
        (owners[None, :] == owners[:, None]) & (block_order[None, :] < block_order[:, None]), axis=1
    )
    targets = owners * send_most + block_ranks
    slot_order = jnp.arange(slot_count, dtype=jnp.int32)
    slot_hits = targets[None, :] == slot_order[:, None]
    picked = jnp.sum(jnp.where(slot_hits, block_order[None, :], 0), axis=1)
    filled = jnp.any(slot_hits, axis=1)
    sent_labels = jnp.where(filled, labels[picked], -1).reshape(seq_count, send_most)

    def outgoing(blocks):
        return jnp.where(filled[:, None, None], blocks[picked], 0).reshape(
            seq_count, send_most, BLOCK, blocks.shape[2]
        )

    def into_clusters(received, fetch_from, loaded):
        flat_rows = received.reshape(slot_count, BLOCK, received.shape[3])
        gathered = jnp.where(loaded[:, None, None], flat_rows[fetch_from], 0)
        return gathered.reshape(CLUS_DEV, capacity * BLOCK, received.shape[3])

    def from_clusters(results, places, present):
        flat_rows = results.reshape(slot_count, BLOCK, results.shape[2])
        gathered = jnp.where(present[:, None, None], flat_rows[jnp.maximum(places, 0)], 0)
        return gathered.reshape(seq_count, send_most, BLOCK, results.shape[2])

    def to_blocks(back_rows):
        flat_rows = back_rows.reshape(slot_count, BLOCK, back_rows.shape[3])
        return flat_rows[targets].reshape(token_count, back_rows.shape[3])

    pair_blocks = jnp.concatenate([routed_query, routed_value], axis=1).reshape(
        block_count, BLOCK, 2 * HEAD
    )
    arrived, arrived_labels = (
        lax.all_to_all(outgoing(pair_blocks), "seq", split_axis=0, concat_axis=0, tiled=True),
        lax.all_to_all(sent_labels, "seq", split_axis=0, concat_axis=0, tiled=True),
    )
    flat_labels = arrived_labels.reshape(slot_count)
    present = flat_labels >= 0
    inner_index = flat_labels - position * CLUS_DEV
    same_label = (flat_labels[None, :] == flat_labels[:, None]) & present[None, :]
    earlier = slot_order[None, :] < slot_order[:, None]
    label_ranks = jnp.sum(same_label & earlier, axis=1)
    places = jnp.where(present, inner_index * capacity + label_ranks, -1).astype(jnp.int32)
    grid_hits = places[None, :] == slot_order[:, None]
    fetch_from = jnp.sum(jnp.where(grid_hits, slot_order[None, :], 0), axis=1)
    loaded = jnp.any(grid_hits, axis=1)
    places, present, fetch_from, loaded = (places, present, fetch_from, loaded)
    held_blocks = into_clusters(arrived, fetch_from, loaded)
    forward = lax.map(forward_pass, held_blocks)
    back_out = lax.all_to_all(
        from_clusters(forward, places, present), "seq", split_axis=0, concat_axis=0, tiled=True
    )
    routed_out = to_blocks(back_out)
    tangent_blocks = routed_tangent.reshape(block_count, BLOCK, HEAD)
    arrived_tangent = lax.all_to_all(
        outgoing(tangent_blocks), "seq", split_axis=0, concat_axis=0, tiled=True
    )
    combined = jnp.concatenate(
        [held_blocks, into_clusters(arrived_tangent, fetch_from, loaded)], axis=2
    )
    results = lax.map(full_pass, combined)
    back_grads = lax.all_to_all(
        from_clusters(results[:, :, HEAD:], places, present),
        "seq",
        split_axis=0,
        concat_axis=0,
        tiled=True,
    )
    grads_all = to_blocks(back_grads)
    routed_dq = grads_all[:, :HEAD]
    routed_dv = grads_all[:, HEAD:]
    attended = jnp.concatenate([outputs, routed_out], axis=1)
    query_all = jnp.concatenate([local_dq, routed_dq], axis=1)
    value_all = jnp.concatenate([local_dv, routed_dv], axis=1)
    partial_sums = contract(query_all, shared_weight, 1, 1) + contract(
        value_all, value_weight, 1, 1
    )
    token_grads = lax.psum_scatter(partial_sums, "wide", scatter_dimension=1, tiled=True).astype(
        jnp.bfloat16
    )
    grad_scale = 1.0 / math.sqrt(seq_tokens)
    summed = lax.psum_scatter(
        jnp.concatenate(
            [
                contract(tokens, query_all, 0, 0),
                contract(tokens, value_all, 0, 0),
                contract(cotangent, attended, 0, 0),
            ],
            axis=1,
        )
        * grad_scale,
        "seq",
        scatter_dimension=0,
        tiled=True,
    )
    pair_width = 2 * HEAD
    return (
        token_grads,
        summed[:, :pair_width],
        summed[:, pair_width : 2 * pair_width],
        summed[:, 2 * pair_width :].T,
    )


def solution(mesh):
    placed = (
        P("seq", None),
        P(None, "wide"),
        P(None, "wide"),
        P("wide", None),
        P("seq", None),
        P("wide", "seq"),
    )
    return jax.shard_map(
        on_device,
        mesh=mesh,
        in_specs=placed,
        out_specs=(P("seq", "wide"), P("seq", "wide"), P("seq", "wide"), P("wide", "seq")),
        check_vma=False,
    )
```

profile of v0, /device:TPU:1, one launch (start us, length us, event | category | flops | bytes accessed | tf_op | source)
XLA Modules:
  0.0 646.4 jit_solution(15805127554247743985)
XLA Ops:
  11.6 7.6 %fusion.96 = s32[64]{0:T(128)S(1)} fusion(pred[64]{0:T(512)(128)(4,1)S(1)} %fusion.88, s32[]{:T(128)} %bitcast.10, s32[]{:T(128)} %bitcast.11, s32[]{:T(128)} %bitcast.12, s32[]{:T(128)} %bitcast.13, s32[]{:T(128)} %bitcast.14, s32[]{:T(128)} %bitcast.15, s32[]{:T(128)} %bitcast.16, s32[]{:T(128)} %bitcast.17, s32[]{:T(128)} %bitcast.18, s32[]{:T(128)} %bitcast.19, ...), kind=kLoop, calls=%fused_computation.210 | loop fusion | flops 1664 | bytes 624 | tf_op jit(solution)/shard_map/jit(_where)/select_n | solution.py:197
  19.9 9.6 %all-to-all-start = ((s32[32,1,2]{2,1,0:T(1,128)}), s32[32,1,2]{2,1,0:T(1,128)S(1)}, u32[]{:S(2)}, u32[]{:S(2)}) async-start(s32[32,1,2]{2,1,0:T(1,128)} %bitcast.22), calls=%async_computation | async-start | bytes 32768 | tf_op jit(solution)/shard_map/all_to_all | solution.py:223
  30.8 3.0 convolution_convert_fusion.3
  34.7 2.3 gather_fusion.2
  37.0 3.1 broadcast_select_fusion.3
  40.1 7.4 %all-to-all-start.2 = ((bf16[32,2,128,128]{3,2,1,0:T(8,128)(2,1)}), bf16[32,2,128,128]{3,2,1,0:T(8,128)(2,1)}, u32[]{:S(2)}, u32[]{:S(2)}) async-start(bf16[32,2,128,128]{3,2,1,0:T(8,128)(2,1)} %broadcast_select_fusion.3), calls=%async_computation.2 | async-start | bytes 4194304 | tf_op jit(solution)/shard_map/all_to_all | solution.py:243
  53.8 2.3 copy.83
  56.1 4.0 gather_fusion
  60.1 4.6 broadcast_select_fusion
  64.7 11.3 %all-to-all-done.2 = bf16[32,2,128,128]{3,2,1,0:T(8,128)(2,1)} async-done(((bf16[32,2,128,128]{3,2,1,0:T(8,128)(2,1)}), bf16[32,2,128,128]{3,2,1,0:T(8,128)(2,1)}, u32[]{:S(2)}, u32[]{:S(2)}) %all-to-all-start.2) | async-done | bytes 2097184 | tf_op jit(solution)/shard_map/all_to_all | solution.py:243
  75.9 5.3 all-to-all-start.1
  82.7 3.5 collective-permute-start
  101.3 28.8 %collective-permute-done = bf16[256,256]{0,1:T(8,128)(2,1)} collective-permute-done((bf16[256,256]{0,1:T(8,128)(2,1)}, bf16[256,256]{0,1:T(8,128)(2,1)}, u32[]{:S(2)}, u32[]{:S(2)}) %collective-permute-start) | collective-permute-done | bytes 131104 | tf_op jit(solution)/shard_map/ppermute | solution.py:21
  134.6 3.8 gather_fusion.3
  138.5 4.4 bitcast_select_fusion.1
  142.9 5.2 gather_fusion.1
  148.1 5.3 bitcast_select_fusion
  153.4 33.1 %while.48 = (s32[]{:T(128)}, bf16[8,1024,128]{2,1,0:T(8,128)(2,1)}, bf16[8,1024,256]{2,1,0:T(8,128)(2,1)}) while((s32[]{:T(128)}, bf16[8,1024,128]{2,1,0:T(8,128)(2,1)}, bf16[8,1024,256]{2,1,0:T(8,128)(2,1)}) %tuple.154), condition=%wide.region_25.26_spmd.clone, body=%wide.region_21.25_spmd.sunk.clone | while | flops 553516032 | bytes 14979133 | solution.py:237
  186.5 3.7 gather_fusion.6
  190.2 3.1 broadcast_select_fusion.2
  193.3 7.9 %all-to-all-start.4 = ((bf16[32,2,128,128]{3,2,1,0:T(8,128)(2,1)}), bf16[32,2,128,128]{3,2,1,0:T(8,128)(2,1)}, u32[]{:S(2)}, u32[]{:S(2)}) async-start(bf16[32,2,128,128]{3,2,1,0:T(8,128)(2,1)} %broadcast_select_fusion.2), calls=%async_computation.5 | async-start | bytes 4194304 | tf_op jit(solution)/shard_map/all_to_all | solution.py:238
  201.3 6.1 pad_maximum_fusion
  207.4 148.9 %while.47 = (s32[]{:T(128)}, bf16[8,1024,384]{2,1,0:T(8,128)(2,1)}, bf16[8,1024,384]{2,1,0:T(8,128)(2,1)}) while((s32[]{:T(128)}, bf16[8,1024,384]{2,1,0:T(8,128)(2,1)}, bf16[8,1024,384]{2,1,0:T(8,128)(2,1)}) %tuple.148), condition=%wide.region_19.20_spmd.clone, body=%wide.region_13.19_spmd.sunk.clone | while | flops 1653473280 | bytes 55668824 | solution.py:249
  209.5 2.3 copy.122
  221.6 2.3 copy.123
  228.1 2.3 copy.122
  240.2 2.3 copy.123
  246.7 2.3 copy.122
  258.9 2.3 copy.123
  265.3 2.3 copy.122
  277.5 2.3 copy.123
  284.0 2.3 copy.122
  296.1 2.3 copy.123
  302.6 2.3 copy.122
  314.7 2.3 copy.123
  321.2 2.3 copy.122
  333.3 2.3 copy.123
  339.8 2.3 copy.122
  351.9 2.3 copy.123
  354.2 2.1 constant_dynamic-update-slice_fusion.6
  356.4 4.5 slice.113
  360.8 5.1 gather_fusion.4
  365.9 4.5 broadcast_select_fusion.1
  370.4 7.4 %all-to-all-start.3 = ((bf16[32,2,128,256]{3,2,1,0:T(8,128)(2,1)}), bf16[32,2,128,256]{3,2,1,0:T(8,128)(2,1)}, u32[]{:S(2)}, u32[]{:S(2)}) async-start(bf16[32,2,128,256]{3,2,1,0:T(8,128)(2,1)} %broadcast_select_fusion.1), calls=%async_computation.3 | async-start | bytes 8388608 | tf_op jit(solution)/shard_map/all_to_all | solution.py:250
  381.9 65.3 %while.49 = (s32[]{:T(128)}, f32[1792,128]{0,1:T(8,128)}, f32[1792,128]{1,0:T(8,128)}, bf16[1536,128]{1,0:T(8,128)(2,1)}, f32[1536,128]{0,1:T(8,128)}, /*index=5...) while((s32[]{:T(128)}, f32[1792,128]{0,1:T(8,128)}, ...), condition=%wide.region_5.6_spmd.clone.clone.clone.clone, body=%wide.region_1.5_spmd.clone.clone.clone.sunk.clone | while | flops 620755456 | bytes 29255732 | solution.py:113
  397.7 2.4 fusion.228
  400.2 2.7 fusion.227
  410.5 2.1 multiply_reduce_fusion.8
  419.5 2.4 fusion.228
  422.0 2.7 fusion.227
  441.3 2.4 fusion.228
  443.7 2.7 fusion.227
  448.1 2.5 copy.77
  451.5 2.2 collective-permute-start.1
  463.9 3.1 gather_fusion.7
  467.0 4.2 convolution_bitcast_fusion
  471.2 3.8 gather_fusion.5
  482.3 2.3 maximum_multiply_fusion
  484.6 3.6 copy.93
  488.3 2.3 fusion.84
  490.7 3.7 convolution_add_fusion.3
  494.4 75.6 %reduce-scatter.7.cloned.1.call-done = f32[32,768]{1,0:T(8,128)} async-done(((f32[1024,768]{1,0:T(8,128)}), f32[32,768]{1,0:T(8,128)}) %reduce-scatter.7.cloned.1.call-update) | async-done | bytes 98320
  571.4 65.8 %reduce-scatter.5.cloned.1.call-done = f32[1536,256]{1,0:T(8,128)} async-done(((f32[1536,1024]{1,0:T(8,128)}), f32[1536,256]{1,0:T(8,128)}) %reduce-scatter.5.cloned.1.call-update) | async-done | bytes 1572880 | tf_op jit(solution)/shard_map/reduce_scatter | solution.py:266
  637.2 2.4 convert_element_type.112
  (320 shorter events, 249.7 us)
Async XLA Ops:
  7.2 40.4 %copy-start = (bf16[1536,1024]{1,0:T(8,128)(2,1)S(1)}, bf16[1536,1024]{1,0:T(8,128)(2,1)}, u32[]{:S(2)}) copy-start(bf16[1536,1024]{1,0:T(8,128)(2,1)} %param.12) | copy-start | bytes 9437188
  9.0 2.6 copy-start.18
  19.9 20.2 %all-to-all-start = ((s32[32,1,2]{2,1,0:T(1,128)}), s32[32,1,2]{2,1,0:T(1,128)S(1)}, u32[]{:S(2)}, u32[]{:S(2)}) async-start(s32[32,1,2]{2,1,0:T(1,128)} %bitcast.22), calls=%async_computation | async-start | bytes 32768 | tf_op jit(solution)/shard_map/all_to_all | solution.py:223
  40.1 35.8 %all-to-all-start.2 = ((bf16[32,2,128,128]{3,2,1,0:T(8,128)(2,1)}), bf16[32,2,128,128]{3,2,1,0:T(8,128)(2,1)}, u32[]{:S(2)}, u32[]{:S(2)}) async-start(bf16[32,2,128,128]{3,2,1,0:T(8,128)(2,1)} %broadcast_select_fusion.3), calls=%async_computation.2 | async-start | bytes 4194304 | tf_op jit(solution)/shard_map/all_to_all | solution.py:243
  47.5 2.8 copy-start.10
  49.7 3.2 copy-start.3
  75.9 67.0 %all-to-all-start.1 = ((bf16[32,2,128,256]{3,2,1,0:T(8,128)(2,1)}), bf16[32,2,128,256]{3,2,1,0:T(8,128)(2,1)}, u32[]{:S(2)}, u32[]{:S(2)}) async-start(bf16[32,2,128,256]{3,2,1,0:T(8,128)(2,1)} %broadcast_select_fusion), calls=%async_computation.1 | async-start | bytes 8388608 | tf_op jit(solution)/shard_map/all_to_all | solution.py:222
  82.7 47.4 %collective-permute-start = (bf16[256,256]{0,1:T(8,128)(2,1)}, bf16[256,256]{0,1:T(8,128)(2,1)}, u32[]{:S(2)}, u32[]{:S(2)}) collective-permute-start(bf16[256,256]{0,1:T(8,128)(2,1)} %pad_maximum_fusion.12), channel_id=1, source_target_pairs={{0,4},{4,8},{8,12},{12,16},{16,20},{20,24},{24,28},{28,32},{32,36}... | collective-permute-start | bytes 393224 | tf_op jit(solution)/shard_map/ppermute | solution.py:21
  95.6 0.6 copy-start.17
  131.1 3.5 copy-start.15
  193.3 177.1 %all-to-all-start.4 = ((bf16[32,2,128,128]{3,2,1,0:T(8,128)(2,1)}), bf16[32,2,128,128]{3,2,1,0:T(8,128)(2,1)}, u32[]{:S(2)}, u32[]{:S(2)}) async-start(bf16[32,2,128,128]{3,2,1,0:T(8,128)(2,1)} %broadcast_select_fusion.2), calls=%async_computation.5 | async-start | bytes 4194304 | tf_op jit(solution)/shard_map/all_to_all | solution.py:238
  214.7 1.1 copy-start.2
  233.3 1.1 copy-start.2
  252.0 1.1 copy-start.2
  270.6 1.1 copy-start.2
  289.2 1.1 copy-start.2
  307.8 1.1 copy-start.2
  326.4 1.1 copy-start.2
  345.0 1.1 copy-start.2
  370.4 11.5 %copy-start.14 = (s32[512]{0:T(512)S(1)}, s32[512]{0:T(512)}, u32[]{:S(2)}) copy-start(s32[512]{0:T(512)} %iota_add_fusion.1) | copy-start | bytes 6148
  370.4 100.8 %all-to-all-start.3 = ((bf16[32,2,128,256]{3,2,1,0:T(8,128)(2,1)}), bf16[32,2,128,256]{3,2,1,0:T(8,128)(2,1)}, u32[]{:S(2)}, u32[]{:S(2)}) async-start(bf16[32,2,128,256]{3,2,1,0:T(8,128)(2,1)} %broadcast_select_fusion.1), calls=%async_computation.3 | async-start | bytes 8388608 | tf_op jit(solution)/shard_map/all_to_all | solution.py:250
  377.8 192.1 %reduce-scatter.7.cloned.1.call-start = ((), (), s32[]{:S(2)}) async-start(), calls=%async_computation.8 | async-start | bytes 3244032
  381.9 73.2 %copy-start.16 = (f32[1792]{0:T(1024)S(1)}, f32[1792]{0:T(1024)}, u32[]{:S(2)}) copy-start(f32[1792]{0:T(1024)} %copy-done.15) | copy-start | bytes 21508
  390.8 1.2 copy-start.1
  412.6 1.2 copy-start.1
  434.4 1.2 copy-start.1
  451.5 7.7 %collective-permute-start.1 = (f32[256,256]{0,1:T(8,128)S(1)}, f32[256,256]{0,1:T(8,128)S(1)}, u32[]{:S(2)}, u32[]{:S(2)}) collective-permute-start(f32[256,256]{0,1:T(8,128)S(1)} %pad_maximum_fusion.11), channel_id=1, source_target_pairs={{4,0},{8,4},{12,8},{16,12},{20,16},{24,20},{28,24},{32,28},{36,32}... | collective-permute-start | bytes 786440 | tf_op jit(solution)/shard_map/ppermute | solution.py:21
  460.2 2.0 copy-start.8
  479.0 2.1 copy-start.4
  479.0 2.1 copy-start.6
  479.0 2.1 copy-start.12
  481.1 1.2 copy-start.9
  488.2 149.0 %reduce-scatter.5.cloned.1.call-start = ((), (), s32[]{:S(2)}) async-start(), calls=%async_computation.7 | async-start | bytes 7864320 | tf_op jit(solution)/shard_map/reduce_scatter | solution.py:266
  488.3 2.3 copy-start.5
  488.3 2.3 copy-start.7
  488.3 2.3 copy-start.11
  488.3 2.3 copy-start.13
Sparse Core Ops, SparseCore 0:
  488.3 81.5 reduce-scatter.6
  572.4 64.7 reduce-scatter.4
where the time goes:
time: 652 us; the launch traced here: 646 us
  waiting for transfers between devices  182 us (28%)
  local copies, waits for them, and re-layouts  179 us (27%)
  matrix products  124 us (19%)
  other arithmetic  102 us (16%)
  starting transfers between devices  43.7 us (7%)
  between operations  14.4 us (2%)
    dot_general x87, matrix products, contract(): lax.dot_general(left_side, right_side, (((left_dim,), (right_dim,)), ((),...  118 us
    unnamed x3, waiting for transfers between devices  75.6 us
    reduce_scatter x1, waiting for transfers between devices, on_device(): lax.psum_scatter(partial_sums, 'wide', scatter_dimension=1, tiled=True)  65.8 us
    dynamic_update_slice x16, local copies, waits for them, and re-layouts, on_device(): results = lax.map(full_pass, combined)  35.1 us
    dynamic_slice x16, local copies, waits for them, and re-layouts, on_device(): results = lax.map(full_pass, combined)  35 us
    ppermute x2, waiting for transfers between devices, shifted(): lax.ppermute(value, axis, [(source, source + steps) for source in range(f...  29.1 us
  transfers between devices with their start and end apart: 9, of which 5 were waited for; matrix products, arithmetic and copies ran while one was open for 49% of the time, Pallas kernels for 0%

commit v1 on v0

v1 whole, which is shorter than its diff:
```python
import functools
import math

import jax
import jax.numpy as jnp
from jax import lax
from jax.experimental import pallas as pl
from jax.experimental.pallas import tpu as pltpu
from jax.sharding import PartitionSpec as P

HEAD = 128
WINDOW = 256
BLOCK = 128
MOST = 8
SLOTS = 16

EPSILON = 1e-06
NEGATIVE = -1e30
TILE = 256


def contract(left_side, right_side, left_dim, right_dim):
    return lax.dot_general(
        left_side,
        right_side,
        (((left_dim,), (right_dim,)), ((), ())),
        preferred_element_type=jnp.float32,
    )


def unit_factor(floats):
    return lax.rsqrt(jnp.mean(floats * floats, axis=-1, keepdims=True) + EPSILON)


def chain(floats, key_grads):
    factor = unit_factor(floats)
    inner_sum = jnp.sum(floats * key_grads, axis=-1, keepdims=True)
    return factor * key_grads - factor**3 / HEAD * floats * inner_sum


def attend(queries, keys, values, tangents, allowed, self_spot):
    head_scale = 1.0 / math.sqrt(HEAD)
    scores = contract(queries, keys, 1, 1) * head_scale
    scores = jnp.where(self_spot, 0.0, scores)
    scores = jnp.where(allowed, scores, NEGATIVE)
    highest = jnp.max(scores, axis=1, keepdims=True)
    weights = jnp.exp(scores - highest)
    probs = weights * (1.0 / jnp.sum(weights, axis=1, keepdims=True))
    probs_half = probs.astype(jnp.bfloat16)
    outputs = contract(probs_half, values, 1, 0)
    prob_grads = contract(tangents, values, 1, 1)
    centre = jnp.sum(probs * prob_grads, axis=1, keepdims=True)
    score_grads = jnp.where(self_spot, 0.0, probs * (prob_grads - centre))
    score_half = (score_grads * head_scale).astype(jnp.bfloat16)
    query_grads = contract(score_half, keys, 1, 0)
    key_grads = contract(score_half, queries, 0, 0)
    value_grads = contract(probs_half, tangents, 0, 0)
    return outputs, query_grads, key_grads, value_grads


def gather_kernel(index_ref, in_ref, out_ref):
    count = out_ref.shape[0]

    def step(spot, carry):
        out_ref[spot] = in_ref[index_ref[spot]]
        return carry

    lax.fori_loop(0, count, step, 0, unroll=8)


def gather_chunks(index, chunks, count):
    return pl.pallas_call(
        gather_kernel,
        out_shape=jax.ShapeDtypeStruct((count,) + chunks.shape[1:], chunks.dtype),
        in_specs=[
            pl.BlockSpec(memory_space=pltpu.SMEM),
            pl.BlockSpec(memory_space=pltpu.VMEM),
        ],
        out_specs=pl.BlockSpec(memory_space=pltpu.VMEM),
        cost_estimate=pl.CostEstimate(flops=0, bytes_accessed=4 << 20, transcendentals=0),
        name="gather_chunks",
    )(index, chunks)


def cluster_kernel(first_ref, data_ref, out_ref, key_buf, query_sums, key_sums, value_sums):
    key_sums[...] = jnp.zeros_like(key_sums)
    value_sums[...] = jnp.zeros_like(value_sums)

    def make_keys(slot, carry):
        rows = pl.ds(pl.multiple_of(slot * BLOCK, BLOCK), BLOCK)
        floats = data_ref[rows, :HEAD].astype(jnp.float32)
        key_buf[rows, :] = (floats * unit_factor(floats)).astype(jnp.bfloat16)
        return carry

    lax.fori_loop(0, SLOTS, make_keys, 0)

    def visit(slot, first, reach):
        width = reach * BLOCK
        begin = jnp.maximum(slot - (reach - 1), 0)
        rows = pl.ds(pl.multiple_of(slot * BLOCK, BLOCK), BLOCK)
        span = pl.ds(pl.multiple_of(begin * BLOCK, BLOCK), width)
        spot = lax.broadcasted_iota(jnp.int32, (BLOCK, width), 1)
        row = lax.broadcasted_iota(jnp.int32, (BLOCK, width), 0) + (slot - begin) * BLOCK
        self_spot = spot == row
        allowed = (spot <= row) & (spot >= (first - begin) * BLOCK)
        outputs, query_grads, key_grads, value_grads = attend(
            data_ref[rows, :HEAD],
            key_buf[span, :],
            data_ref[span, HEAD : 2 * HEAD],
            data_ref[rows, 2 * HEAD :],
            allowed,
            self_spot,
        )
        out_ref[rows, :HEAD] = outputs.astype(jnp.bfloat16)
        query_sums[rows, :] = query_grads
        key_sums[span, :] += key_grads
        value_sums[span, :] += value_grads

    def step(slot, carry):
        first = first_ref[slot]
        count = slot - first + 1

        @pl.when((first >= 0) & (count <= 2))
        def _():
            visit(slot, first, 2)

        @pl.when((first >= 0) & (count > 2) & (count <= 4))
        def _():
            visit(slot, first, 4)

        @pl.when((first >= 0) & (count > 4))
        def _():
            visit(slot, first, MOST)

        return carry

    lax.fori_loop(0, SLOTS, step, 0)

    def finish(slot, carry):
        rows = pl.ds(pl.multiple_of(slot * BLOCK, BLOCK), BLOCK)
        floats = data_ref[rows, :HEAD].astype(jnp.float32)
        total = query_sums[rows, :] + chain(floats, key_sums[rows, :])
        out_ref[rows, HEAD : 2 * HEAD] = total.astype(jnp.bfloat16)
        out_ref[rows, 2 * HEAD :] = value_sums[rows, :].astype(jnp.bfloat16)
        return carry

    lax.fori_loop(0, SLOTS, finish, 0)


def cluster_attention(first, data):
    rows = data.shape[0]
    return pl.pallas_call(
        cluster_kernel,
        out_shape=jax.ShapeDtypeStruct(data.shape, jnp.bfloat16),
        in_specs=[
            pl.BlockSpec(memory_space=pltpu.SMEM),
            pl.BlockSpec(memory_space=pltpu.VMEM),
        ],
        out_specs=pl.BlockSpec(memory_space=pltpu.VMEM),
        scratch_shapes=[
            pltpu.VMEM((rows, HEAD), jnp.bfloat16),
            pltpu.VMEM((rows, HEAD), jnp.float32),
            pltpu.VMEM((rows, HEAD), jnp.float32),
            pltpu.VMEM((rows, HEAD), jnp.float32),
        ],
        cost_estimate=pl.CostEstimate(
            flops=12 << 30, bytes_accessed=4 << 20, transcendentals=1 << 20
        ),
        name="cluster_attention",
    )(first, data)


def band_kernel(place_ref, data_ref, before_ref, after_ref, out_ref, ext, key_buf, query_sums, key_sums, value_sums):
    own = data_ref.shape[0]
    tiles = own // TILE
    ext[:WINDOW, :] = before_ref[...]
    ext[WINDOW : WINDOW + own, :] = data_ref[...]
    ext[WINDOW + own :, :] = after_ref[...]
    key_sums[...] = jnp.zeros_like(key_sums)
    value_sums[...] = jnp.zeros_like(value_sums)

    def make_keys(tile, carry):
        rows = pl.ds(pl.multiple_of(tile * TILE, TILE), TILE)
        floats = ext[rows, :HEAD].astype(jnp.float32)
        key_buf[rows, :] = (floats * unit_factor(floats)).astype(jnp.bfloat16)
        return carry

    lax.fori_loop(0, tiles + 2, make_keys, 0)
    spot = lax.broadcasted_iota(jnp.int32, (TILE, TILE + WINDOW), 1)
    row = lax.broadcasted_iota(jnp.int32, (TILE, TILE + WINDOW), 0)

    def step(tile, carry):
        rows = pl.ds(pl.multiple_of(tile * TILE + WINDOW, TILE), TILE)
        span = pl.ds(pl.multiple_of(tile * TILE, TILE), TILE + WINDOW)
        least = jnp.where((tile == 0) & (place_ref[0] == 0), WINDOW, 0)
        self_spot = spot == row + WINDOW
        allowed = (spot >= row) & (spot <= row + WINDOW) & (spot >= least)
        outputs, query_grads, key_grads, value_grads = attend(
            ext[rows, :HEAD],
            key_buf[span, :],
            ext[span, HEAD : 2 * HEAD],
            ext[rows, 2 * HEAD :],
            allowed,
            self_spot,
        )
        query_sums[rows, :] = query_grads
        key_sums[span, :] += key_grads
        value_sums[span, :] += value_grads

        @pl.when(tile < tiles)
        def _():
            into = pl.ds(pl.multiple_of(tile * TILE, TILE), TILE)
            out_ref[into, :HEAD] = outputs.astype(jnp.bfloat16)

        return carry

    lax.fori_loop(0, jnp.where(place_ref[1] == 1, tiles, tiles + 1), step, 0)

    def finish(tile, carry):
        rows = pl.ds(pl.multiple_of(tile * TILE + WINDOW, TILE), TILE)
        into = pl.ds(pl.multiple_of(tile * TILE, TILE), TILE)
        floats = ext[rows, :HEAD].astype(jnp.float32)
        total = query_sums[rows, :] + chain(floats, key_sums[rows, :])
        out_ref[into, HEAD : 2 * HEAD] = total.astype(jnp.bfloat16)
        out_ref[into, 2 * HEAD :] = value_sums[rows, :].astype(jnp.bfloat16)
        return carry

    lax.fori_loop(0, tiles, finish, 0)


def band_attention(place, data, before, after):
    rows = data.shape[0] + 2 * WINDOW
    return pl.pallas_call(
        band_kernel,
        out_shape=jax.ShapeDtypeStruct(data.shape, jnp.bfloat16),
        in_specs=[pl.BlockSpec(memory_space=pltpu.SMEM)] + [pl.BlockSpec(memory_space=pltpu.VMEM)] * 3,
        out_specs=pl.BlockSpec(memory_space=pltpu.VMEM),
        scratch_shapes=[
            pltpu.VMEM((rows, 3 * HEAD), jnp.bfloat16),
            pltpu.VMEM((rows, HEAD), jnp.bfloat16),
            pltpu.VMEM((rows, HEAD), jnp.float32),
            pltpu.VMEM((rows, HEAD), jnp.float32),
            pltpu.VMEM((rows, HEAD), jnp.float32),
        ],
        cost_estimate=pl.CostEstimate(
            flops=12 << 30, bytes_accessed=4 << 20, transcendentals=1 << 20
        ),
        name="band_attention",
    )(place, data, before, after)


def shifted(value, axis, steps):
    count = lax.axis_size(axis)
    pairs = [(i, i + steps) for i in range(count) if 0 <= i + steps < count]
    return lax.ppermute(value, axis, pairs)


def turned(value, axis, steps):
    count = lax.axis_size(axis)
    return lax.ppermute(value, axis, [(i, (i + steps) % count) for i in range(count)])


def ring_gather(value, axis):
    half = value.shape[0] // 2
    left = turned(value, axis, 1)
    right = turned(value, axis, -1)
    far_top = turned(left[:half], axis, 1)
    far_low = turned(right[half:], axis, -1)
    far = jnp.concatenate([far_top, far_low], axis=0)
    return value, left, right, far


def exchange(value, axis):
    return lax.all_to_all(value, axis, split_axis=0, concat_axis=0, tiled=True)


def route(labels, seq_count, per_device):
    order = jnp.arange(labels.shape[0], dtype=jnp.int32)
    same = labels[None, :] == labels[:, None]
    rank = jnp.sum(same & (order[None, :] < order[:, None]), axis=1).astype(jnp.int32)
    size = jnp.sum(same, axis=1).astype(jnp.int32)
    rating = size * 4096 - labels
    start = jnp.sum(rating[None, :] > rating[:, None], axis=1).astype(jnp.int32)
    owner = start // per_device
    base = jnp.min(
        jnp.where(owner[None, :] == owner[:, None], start[None, :], labels.shape[0]), axis=1
    ).astype(jnp.int32)
    target = owner * SLOTS + start + rank - base
    head = owner * SLOTS + start - base
    spots = jnp.arange(seq_count * SLOTS, dtype=jnp.int32)
    hits = target[None, :] == spots[:, None]
    picked = jnp.sum(jnp.where(hits, order[None, :], 0), axis=1).astype(jnp.int32)
    first = jnp.sum(jnp.where(hits, head[None, :] % SLOTS + 1, 0), axis=1).astype(jnp.int32) - 1
    return target, picked, first


def on_device(tokens, shared_weight, value_weight, output_weight, cotangent, block_clusters):
    seq_count = lax.axis_size("seq")
    wide_count = lax.axis_size("wide")
    position = lax.axis_index("seq")
    here = lax.axis_index("wide")
    token_count, width = tokens.shape
    block_count = token_count // BLOCK
    piece = BLOCK // seq_count

    routed_pair = jnp.concatenate([shared_weight[:, HEAD:], value_weight[:, HEAD:]], axis=1)
    routed = jnp.concatenate(
        [contract(tokens, routed_pair, 1, 0), contract(cotangent, output_weight[HEAD:], 1, 1)],
        axis=1,
    ).astype(jnp.bfloat16)
    leaving = routed.reshape(block_count, seq_count, piece, 3 * HEAD).transpose(1, 0, 2, 3)
    labels = lax.all_gather(block_clusters[0], "seq", axis=0, tiled=True)
    target, picked, first = route(labels, seq_count, block_count)
    middle = exchange(leaving, "seq").reshape(seq_count * block_count, piece, 3 * HEAD)
    sent = gather_chunks(picked, middle, seq_count * SLOTS)
    arrived = exchange(sent.reshape(seq_count, SLOTS, piece, 3 * HEAD), "seq")
    held = arrived.transpose(1, 0, 2, 3).reshape(SLOTS * BLOCK, 3 * HEAD)
    own_first = lax.dynamic_slice_in_dim(first, position * SLOTS, SLOTS, 0)
    results = cluster_attention(own_first, held)
    turned_back = results.reshape(SLOTS, seq_count, piece, 3 * HEAD).transpose(1, 0, 2, 3)
    middle_back = exchange(turned_back, "seq").reshape(seq_count * SLOTS, piece, 3 * HEAD)
    homeward = gather_chunks(target, middle_back, seq_count * block_count)
    home = exchange(homeward.reshape(seq_count, block_count, piece, 3 * HEAD), "seq")
    routed_all = home.transpose(1, 0, 2, 3).reshape(token_count, 3 * HEAD)

    local_pair = jnp.concatenate([shared_weight[:, :HEAD], value_weight[:, :HEAD]], axis=1)
    local = jnp.concatenate(
        [contract(tokens, local_pair, 1, 0), contract(cotangent, output_weight[:HEAD], 1, 1)],
        axis=1,
    ).astype(jnp.bfloat16)
    before = shifted(local[token_count - WINDOW :], "seq", 1)
    after = shifted(local[:WINDOW], "seq", -1)
    place = jnp.stack([position, (position == seq_count - 1).astype(jnp.int32)])
    local_all = band_attention(place, local, before, after)

    weights = jnp.concatenate([shared_weight, value_weight], axis=1)
    pieces = weights.reshape(wide_count, width // wide_count, weights.shape[1])
    columns = exchange(pieces, "wide")

    def input_part(grads, offset):
        total = None
        for steps, part in zip((0, 1, -1, 2), ring_gather(grads, "wide")):
            owner = (here - steps) % wide_count
            rows = lax.dynamic_slice_in_dim(columns, owner, 1, 0)[0]
            rows = jnp.concatenate(
                [rows[:, offset : offset + HEAD], rows[:, 2 * HEAD + offset : 3 * HEAD + offset]],
                axis=1,
            )
            term = contract(part, rows, 1, 1)
            total = term if total is None else total + term
        return total

    grad_scale = 1.0 / math.sqrt(seq_count * token_count)

    def weight_part(rows):
        terms = jnp.concatenate(
            [contract(tokens, rows[:, HEAD:], 0, 0), contract(cotangent, rows[:, :HEAD], 0, 0)],
            axis=1,
        )
        terms = (terms * grad_scale).astype(jnp.bfloat16)
        terms = exchange(terms.reshape(seq_count, width // seq_count, 3 * HEAD), "seq")
        return jnp.sum(terms.astype(jnp.float32), axis=0)

    local_weights = weight_part(local_all)
    routed_weights = weight_part(routed_all)
    token_grads = (
        input_part(local_all[:, HEAD:], 0) + input_part(routed_all[:, HEAD:], HEAD)
    ).astype(jnp.bfloat16)

    def paired(low, high):
        return jnp.concatenate(
            [local_weights[:, low:high], routed_weights[:, low:high]], axis=1
        )

    return (
        token_grads,
        paired(0, HEAD),
        paired(HEAD, 2 * HEAD),
        paired(2 * HEAD, 3 * HEAD).T,
    )


def solution(mesh):
    placed = (
        P("seq", None),
        P(None, "wide"),
        P(None, "wide"),
        P("wide", None),
        P("seq", None),
        P("wide", "seq"),
    )
    return jax.shard_map(
        on_device,
        mesh=mesh,
        in_specs=placed,
        out_specs=(P("seq", "wide"), P("seq", "wide"), P("seq", "wide"), P("wide", "seq")),
        check_vma=False,
    )
```

time: 652 us -> 276 us (0.42)
  waiting for transfers between devices: 182 us -> 36.4 us
  local copies, waits for them, and re-layouts: 179 us -> 57.9 us
  matrix products: 124 us -> 35.6 us
  other arithmetic: 102 us -> 16.6 us
  Pallas kernels: 0 us -> 33.5 us
  starting transfers between devices: 43.7 us -> 68.8 us
  blocking collectives: 0 us -> 22.6 us
  between operations: 14.4 us -> 1.86 us
    dot_general x87 -> x16, matrix products: 118 us -> 35.6 us  [contract(): lax.dot_general(left_side, right_side, (((left_dim,), (right_dim,)), ((),...]
    unnamed x3 -> x0, waiting for transfers between devices: 75.6 us -> none
    reduce_scatter x1 -> x0, waiting for transfers between devices: 65.8 us -> none  [on_device(): lax.psum_scatter(partial_sums, 'wide', scatter_dimension=1, tiled=True)]
    dynamic_slice x25 -> x1, local copies, waits for them, and re-layouts: 46.1 us -> 0.59 us  [on_device(): own_first = lax.dynamic_slice_in_dim(first, position * SLOTS, SLOTS, 0)]
    dynamic_update_slice x22 -> x0, local copies, waits for them, and re-layouts: 41 us -> none  [the longest x16 35.1 us: on_device(): results = lax.map(full_pass, combined)]
    select_n x12 -> x1, other arithmetic: 34 us -> 0.01 us  [route(): owner = start // per_device]
    pallas_call x0 -> x4, Pallas kernels: none -> 33.5 us  [the longest x1 14.9 us: cluster_attention(): pl.pallas_call(cluster_kernel, out_shape=jax.ShapeDtypeStruct(data.shape,...]
    gather x9 -> x0, local copies, waits for them, and re-layouts: 32.8 us -> none  [the longest x2 8.98 us: into_clusters(): gathered = jnp.where(loaded[:, None, None], flat_rows[fetch_from], 0)]
  transfers between devices with their start and end apart: 9 -> 17, of which waited for: 5 -> 7; matrix products, arithmetic and copies ran while one was open for 49% -> 33% of each run, Pallas kernels for 0% -> 11%
where the time goes in v1:
time: 276 us; the launch traced here: 273 us
  starting transfers between devices  68.8 us (25%)
  local copies, waits for them, and re-layouts  57.9 us (21%)
  waiting for transfers between devices  36.4 us (13%)
  matrix products  35.6 us (13%)
  Pallas kernels  33.5 us (12%)
  blocking collectives  22.6 us (8%)
  other arithmetic  16.6 us (6%)
    all_to_all x7, starting transfers between devices, exchange(): return lax.all_to_all(value, axis, split_axis=0, concat_axis=0, tiled=True)  51.3 us
    dot_general x16, matrix products, contract(): lax.dot_general(left_side, right_side, (((left_dim,), (right_dim,)), ((),...  35.6 us
    all_gather x1, blocking collectives, on_device(): labels = lax.all_gather(block_clusters[0], 'seq', axis=0, tiled=True)  22.6 us
    ppermute x8, waiting for transfers between devices, turned(): lax.ppermute(value, axis, [(i, (i + steps) % count) for i in range(count)])  20.1 us
    all_to_all x7, waiting for transfers between devices, exchange(): return lax.all_to_all(value, axis, split_axis=0, concat_axis=0, tiled=True)  16.2 us
    pallas_call x1, Pallas kernels, cluster_attention(): pl.pallas_call(cluster_kernel, out_shape=jax.ShapeDtypeStruct(data.shape,...  14.9 us
    pallas_call x1, Pallas kernels, band_attention(): pl.pallas_call(band_kernel, out_shape=jax.ShapeDtypeStruct(data.shape, jn...  12.3 us
    ppermute x8, starting transfers between devices, turned(): lax.ppermute(value, axis, [(i, (i + steps) % count) for i in range(count)])  12 us
  transfers between devices with their start and end apart: 17, of which 7 were waited for; matrix products, arithmetic and copies ran while one was open for 33% of the time, Pallas kernels for 11%

profile of v1, /device:TPU:1, one launch (start us, length us, event | category | flops | bytes accessed | tf_op | source)
XLA Modules:
  0.0 273.3 jit_solution(6222595276958314576)
XLA Ops:
  0.6 2.2 fusion.74
  2.8 1.9 fusion.5
  4.8 2.3 copy.40
  7.1 2.4 concatenate.86
  9.5 2.9 %convolution_convert_fusion.2 = bf16[1536,128]{1,0:T(8,128)(2,1)S(1)} fusion(bf16[1536,1024]{1,0:T(8,128)(2,1)} %param.10, bf16[256,1024]{1,0:T(8,128)(2,1)} %param.9), kind=kOutput, calls=%fused_computation.12 | convolution fusion | flops 402849792 | bytes 3801088 | tf_op jit(solution)/shard_map/dot_general | solution.py:23
  13.1 1.4 copy.41
  14.5 9.8 %all-to-all-start.1 = ((bf16[32,12,4,384]{3,2,1,0:T(4,128)(2,1)}), bf16[32,12,4,384]{3,2,1,0:T(4,128)(2,1)}, u32[]{:S(2)}, u32[]{:S(2)}) async-start(bf16[32,12,4,384]{3,2,1,0:T(4,128)(2,1)} %copy.41), calls=%async_computation.1 | async-start | bytes 2359296 | tf_op jit(solution)/shard_map/all_to_all | solution.py:274
  25.7 22.6 %all-reduce = s32[384]{0:T(512)S(1)} all-reduce(s32[384]{0:T(512)S(1)} %bitcast_dynamic-update-slice_fusion), channel_id=2, replica_groups=mesh['seq'=32,'wide'=4] {'seq'}, use_global_device_ids=true, to_apply=%add | all-reduce | flops 384 | bytes 3072 | tf_op jit(solution)/shard_map/all_gather | solution.py:312
  50.0 3.3 %gather_chunks.2 = bf16[512,4,384]{2,1,0:T(4,128)(2,1)} custom-call(s32[512]{0:T(512)} %get-tuple-element.4.index_ref, bf16[384,4,384]{2,1,0:T(4,128)(2,1)} %bitcast.13.in_ref), custom_call_target="tpu_custom_call" | custom-call | bytes 4194304 | tf_op jit(solution)/shard_map/gather_chunks/pallas_call | solution.py:72
  53.3 7.7 %all-to-all-start.2 = ((bf16[32,16,4,384]{3,2,1,0:T(4,128)(2,1)}), bf16[32,16,4,384]{3,2,1,0:T(4,128)(2,1)}, u32[]{:S(2)}, u32[]{:S(2)}) async-start(bf16[32,16,4,384]{3,2,1,0:T(4,128)(2,1)} %bitcast.56), calls=%async_computation.2 | async-start | bytes 3145728 | tf_op jit(solution)/shard_map/all_to_all | solution.py:274
  61.1 2.9 %convolution_convert_fusion.3 = bf16[1536,128]{1,0:T(8,128)(2,1)S(1)} fusion(bf16[1536,1024]{1,0:T(8,128)(2,1)} %param.10, bf16[256,1024]{1,0:T(8,128)(2,1)} %param.9), kind=kOutput, calls=%fused_computation.13 | convolution fusion | flops 402849792 | bytes 3801088 | tf_op jit(solution)/shard_map/dot_general | solution.py:23
  66.7 3.5 %collective-permute-start = (bf16[256,384]{1,0:T(8,128)(2,1)}, bf16[256,384]{1,0:T(8,128)(2,1)}, u32[]{:S(2)}, u32[]{:S(2)}) collective-permute-start(bf16[256,384]{1,0:T(8,128)(2,1)} %get-tuple-element.9), channel_id=1, source_target_pairs={{0,4},{4,8},{8,12},{12,16},{16,20},{20,24},{24,28},{28,32},{32,36}... | collective-permute-start | bytes 589832 | tf_op jit(solution)/shard_map/ppermute | solution.py:255
  70.2 1.9 collective-permute-start.1
  73.4 2.3 pad_maximum_fusion.1
  76.8 7.0 %all-to-all-done.2 = bf16[32,16,4,384]{3,2,1,0:T(4,128)(2,1)} async-done(((bf16[32,16,4,384]{3,2,1,0:T(4,128)(2,1)}), bf16[32,16,4,384]{3,2,1,0:T(4,128)(2,1)}, u32[]{:S(2)}, u32[]{:S(2)}) %all-to-all-start.2) | async-done | bytes 1572896 | tf_op jit(solution)/shard_map/all_to_all | solution.py:274
  83.8 4.4 %all-to-all-start = ((bf16[4,256,512]{2,1,0:T(8,128)(2,1)}), bf16[4,256,512]{2,1,0:T(8,128)(2,1)}, u32[]{:S(2)}, u32[]{:S(2)}) async-start(bf16[4,256,512]{2,1,0:T(8,128)(2,1)} %bitcast.59), calls=%async_computation | async-start | bytes 2097152 | tf_op jit(solution)/shard_map/all_to_all | solution.py:274
  88.3 3.3 %copy.42 = bf16[16,32,4,384]{3,2,1,0:T(4,128)(2,1)} copy(bf16[16,32,4,384]{3,2,0,1:T(4,128)(2,1)} %bitcast.15) | data formatting | bytes 3145728 | tf_op jit(solution)/shard_map/transpose | solution.py:317
  91.6 3.7 %reshape.105.data_ref = bf16[2048,384]{1,0:T(8,128)(2,1)} reshape(bf16[16,32,4,384]{3,2,1,0:T(4,128)(2,1)} %copy.42) | data formatting | bytes 3145728 | tf_op jit(solution)/shard_map/reshape | solution.py:317
  95.3 14.9 %cluster_attention.1 = bf16[2048,384]{1,0:T(8,128)(2,1)} custom-call(s32[16]{0:T(128)} %dynamic_slice.23.first_ref, bf16[2048,384]{1,0:T(8,128)(2,1)} %reshape.105.data_ref), custom_call_target="tpu_custom_call" | custom-call | flops 12884901888 | bytes 4194304 | tf_op jit(solution)/shard_map/cluster_attention/pallas_call | solution.py:152
  110.1 3.9 %reshape.106 = bf16[16,32,4,384]{3,2,1,0:T(4,128)(2,1)} reshape(bf16[2048,384]{1,0:T(8,128)(2,1)} %cluster_attention.1) | data formatting | bytes 3145728 | tf_op jit(solution)/shard_map/reshape | solution.py:320
  114.0 3.4 %copy.52 = bf16[16,32,4,384]{3,2,0,1:T(4,128)(2,1)} copy(bf16[16,32,4,384]{3,2,1,0:T(4,128)(2,1)} %reshape.106) | data formatting | bytes 3145728 | tf_op jit(solution)/shard_map/reshape | solution.py:320
  117.4 13.0 %all-to-all-start.3 = ((bf16[32,16,4,384]{3,2,1,0:T(4,128)(2,1)}), bf16[32,16,4,384]{3,2,1,0:T(4,128)(2,1)}, u32[]{:S(2)}, u32[]{:S(2)}) async-start(bf16[32,16,4,384]{3,2,1,0:T(4,128)(2,1)} %bitcast.57), calls=%async_computation.3 | async-start | bytes 3145728 | tf_op jit(solution)/shard_map/all_to_all | solution.py:274
  130.5 12.3 %band_attention.1 = bf16[1536,384]{1,0:T(8,128)(2,1)} custom-call(s32[2]{0:T(128)} %pad_add_fusion.place_ref, bf16[1536,384]{1,0:T(8,128)(2,1)} %pad_maximum_fusion.data_ref, bf16[256,384]{1,0:T(8,128)(2,1)} %collective-permute-done.before_ref, bf16[256,384]{1,0:T(8,128)(2,1)} %collective-permute-done.1.after_ref), custom_call_target="tpu_custom_call" | custom-call | flops 12884901888 | bytes 4194304 | tf_op jit(solution)/shard_map/band_attention/pallas_call | solution.py:233
  142.7 3.4 %convolution_bitcast_fusion.3 = f32[1024,128]{0,1:T(8,128)} fusion(bf16[1536,1024]{1,0:T(8,128)(2,1)} %param.10, bf16[1536,384]{1,0:T(8,128)(2,1)} %band_attention.1), kind=kOutput, calls=%fused_computation.29 | convolution fusion | flops 402653184 | bytes 4063232 | tf_op jit(solution)/shard_map/dot_general | solution.py:23
  146.2 2.1 copy.46
  148.2 3.2 %convolution_bitcast_fusion.1 = f32[1024,256]{0,1:T(8,128)} fusion(bf16[1536,1024]{1,0:T(8,128)(2,1)S(1)} %copy-done, bf16[1536,384]{1,0:T(8,128)(2,1)} %band_attention.1), kind=kOutput, calls=%fused_computation.25 | convolution fusion | flops 805306368 | bytes 4980736 | tf_op jit(solution)/shard_map/dot_general | solution.py:23
  151.4 2.6 copy.45
  153.9 2.5 fusion.7
  156.4 7.5 %all-to-all-start.5 = ((bf16[32,32,384]{2,1,0:T(8,128)(2,1)}), bf16[32,32,384]{2,1,0:T(8,128)(2,1)}, u32[]{:S(2)}, u32[]{:S(2)}) async-start(bf16[32,32,384]{2,1,0:T(8,128)(2,1)} %fusion.7), calls=%async_computation.5 | async-start | bytes 1572864 | tf_op jit(solution)/shard_map/all_to_all | solution.py:274
  164.0 2.1 slice.158
  166.1 2.8 %collective-permute-start.3 = (bf16[1536,256]{1,0:T(8,128)(2,1)}, bf16[1536,256]{1,0:T(8,128)(2,1)}, u32[]{:S(2)}, u32[]{:S(2)}) collective-permute-start(bf16[1536,256]{1,0:T(8,128)(2,1)} %slice.158), channel_id=1, source_target_pairs={{0,3},{1,0},{2,1},{3,2},{4,7},{5,4},{6,5},{7,6},{8,11},{9,8},{10,9... | collective-permute-start | bytes 2359304 | tf_op jit(solution)/shard_map/ppermute | solution.py:260
  168.9 2.1 dynamic-slice_bitcast_fusion.1
  171.0 3.1 %gather_chunks.3 = bf16[384,4,384]{2,1,0:T(4,128)(2,1)} custom-call(s32[384]{0:T(512)} %copy-done.29, bf16[512,4,384]{2,1,0:T(4,128)(2,1)} %bitcast.17.in_ref), custom_call_target="tpu_custom_call" | custom-call | bytes 4194304 | tf_op jit(solution)/shard_map/gather_chunks/pallas_call | solution.py:72
  174.1 4.2 %all-to-all-done.5 = bf16[32,32,384]{2,1,0:T(8,128)(2,1)} async-done(((bf16[32,32,384]{2,1,0:T(8,128)(2,1)}), bf16[32,32,384]{2,1,0:T(8,128)(2,1)}, u32[]{:S(2)}, u32[]{:S(2)}) %all-to-all-start.5) | async-done | bytes 786464 | tf_op jit(solution)/shard_map/all_to_all | solution.py:274
  178.2 4.4 %all-to-all-start.4 = ((bf16[32,12,4,384]{3,2,1,0:T(4,128)(2,1)}), bf16[32,12,4,384]{3,2,1,0:T(4,128)(2,1)}, u32[]{:S(2)}, u32[]{:S(2)}) async-start(bf16[32,12,4,384]{3,2,1,0:T(4,128)(2,1)} %bitcast.58), calls=%async_computation.4 | async-start | bytes 2359296 | tf_op jit(solution)/shard_map/all_to_all | solution.py:274
  182.7 1.6 fusion.79
  184.3 1.6 fusion.76
  186.0 1.6 fusion.77
  188.3 1.3 convert_reduce_fusion.1
  190.2 1.8 slice.166
  192.0 2.8 %collective-permute-start.5 = (bf16[768,256]{1,0:T(8,128)(2,1)}, bf16[768,256]{1,0:T(8,128)(2,1)S(1)}, u32[]{:S(2)}, u32[]{:S(2)}) collective-permute-start(bf16[768,256]{1,0:T(8,128)(2,1)} %slice.166), channel_id=1, source_target_pairs={{0,3},{1,0},{2,1},{3,2},{4,7},{5,4},{6,5},{7,6},{8,11},{9,8},{10,9... | collective-permute-start | bytes 1179656 | tf_op jit(solution)/shard_map/ppermute | solution.py:260
  194.8 1.8 slice.165
  196.6 4.3 %all-to-all-done.4 = bf16[32,12,4,384]{3,2,1,0:T(4,128)(2,1)} async-done(((bf16[32,12,4,384]{3,2,1,0:T(4,128)(2,1)}), bf16[32,12,4,384]{3,2,1,0:T(4,128)(2,1)}, u32[]{:S(2)}, u32[]{:S(2)}) %all-to-all-start.4) | async-done | bytes 1179680 | tf_op jit(solution)/shard_map/all_to_all | solution.py:274
  200.9 2.8 %copy.44 = bf16[12,32,4,384]{3,2,1,0:T(4,128)(2,1)} copy(bf16[12,32,4,384]{3,2,0,1:T(4,128)(2,1)} %bitcast.19) | data formatting | bytes 2359296 | tf_op jit(solution)/shard_map/transpose | solution.py:324
  203.7 3.2 %reshape.109 = bf16[1536,384]{1,0:T(8,128)(2,1)} reshape(bf16[12,32,4,384]{3,2,1,0:T(4,128)(2,1)} %copy.44) | data formatting | bytes 2359296 | tf_op jit(solution)/shard_map/reshape | solution.py:324
  206.9 3.5 %convolution_bitcast_fusion.2 = f32[1024,128]{0,1:T(8,128)} fusion(bf16[1536,1024]{1,0:T(8,128)(2,1)} %param.10, bf16[1536,384]{1,0:T(8,128)(2,1)} %reshape.109), kind=kOutput, calls=%fused_computation.28 | convolution fusion | flops 402653184 | bytes 4063232 | tf_op jit(solution)/shard_map/dot_general | solution.py:23
  210.4 2.0 convolution_bitcast_fusion
  212.4 2.0 copy.48
  214.4 2.5 copy.47
  217.0 2.5 fusion.8
  219.5 4.4 %all-to-all-start.6 = ((bf16[32,32,384]{2,1,0:T(8,128)(2,1)}), bf16[32,32,384]{2,1,0:T(8,128)(2,1)}, u32[]{:S(2)}, u32[]{:S(2)}) async-start(bf16[32,32,384]{2,1,0:T(8,128)(2,1)} %fusion.8), calls=%async_computation.6 | async-start | bytes 1572864 | tf_op jit(solution)/shard_map/all_to_all | solution.py:274
  223.9 2.8 %fusion.37 = f32[1536,256]{1,0:T(8,128)} fusion(bf16[1536,256]{1,0:T(8,128)(2,1)} %collective-permute-done.3, bf16[256,128]{1,0:T(8,128)(2,1)} %get-tuple-element.29, bf16[256,128]{1,0:T(8,128)(2,1)} %get-tuple-element.26), kind=kOutput, calls=%fused_computation.73 | convolution fusion | flops 201588736 | bytes 2490368 | tf_op jit(solution)/shard_map/dot_general | solution.py:23
  226.7 2.7 fusion.33
  229.5 2.6 fusion.9
  233.1 2.8 %collective-permute-start.7 = (bf16[1536,256]{1,0:T(8,128)(2,1)}, bf16[1536,256]{1,0:T(8,128)(2,1)}, u32[]{:S(2)}, u32[]{:S(2)}) collective-permute-start(bf16[1536,256]{1,0:T(8,128)(2,1)} %slice.169), channel_id=1, source_target_pairs={{0,3},{1,0},{2,1},{3,2},{4,7},{5,4},{6,5},{7,6},{8,11},{9,8},{10,9... | collective-permute-start | bytes 2359304 | tf_op jit(solution)/shard_map/ppermute | solution.py:260
  235.9 1.6 fusion.44
  238.2 1.4 convert_reduce_fusion
  240.9 11.9 %collective-permute-done.7 = bf16[1536,256]{1,0:T(8,128)(2,1)} collective-permute-done((bf16[1536,256]{1,0:T(8,128)(2,1)}, bf16[1536,256]{1,0:T(8,128)(2,1)}, u32[]{:S(2)}, u32[]{:S(2)}) %collective-permute-start.7) | collective-permute-done | bytes 786464 | tf_op jit(solution)/shard_map/ppermute | solution.py:260
  253.8 3.5 %collective-permute-start.9 = (bf16[768,256]{1,0:T(8,128)(2,1)S(1)}, bf16[768,256]{1,0:T(8,128)(2,1)S(1)}, u32[]{:S(2)}, u32[]{:S(2)}) collective-permute-start(bf16[768,256]{1,0:T(8,128)(2,1)S(1)} %slice.177), channel_id=1, source_target_pairs={{0,3},{1,0},{2,1},{3,2},{4,7},{5,4},{6,5},{7,6},{8,11},{9,8},{10,9... | collective-permute-start | bytes 1179656 | tf_op jit(solution)/shard_map/ppermute | solution.py:260
  259.0 1.6 convolution_add_fusion.1
  260.6 4.0 %collective-permute-done.9 = bf16[768,256]{1,0:T(8,128)(2,1)S(1)} collective-permute-done((bf16[768,256]{1,0:T(8,128)(2,1)S(1)}, bf16[768,256]{1,0:T(8,128)(2,1)S(1)}, u32[]{:S(2)}, u32[]{:S(2)}) %collective-permute-start.9) | collective-permute-done | bytes 393248 | tf_op jit(solution)/shard_map/ppermute | solution.py:260
  264.6 4.2 %collective-permute-done.8 = bf16[768,256]{1,0:T(8,128)(2,1)S(1)} collective-permute-done((bf16[768,256]{1,0:T(8,128)(2,1)S(1)}, bf16[768,256]{1,0:T(8,128)(2,1)S(1)}, u32[]{:S(2)}, u32[]{:S(2)}) %collective-permute-start.8) | collective-permute-done | bytes 393248 | tf_op jit(solution)/shard_map/ppermute | solution.py:260
  269.3 1.7 fusion
  271.9 1.4 fusion.4
  (106 shorter events, 16.5 us)
Async XLA Ops:
  0.6 2.2 copy-start
  9.5 3.0 %copy-start.10 = (bf16[12,32,4,256]{3,2,1,0:T(4,128)(2,1)S(1)}, bf16[12,32,4,256]{3,2,1,0:T(4,128)(2,1)}, u32[]{:S(2)}) copy-start(bf16[12,32,4,256]{3,2,1,0:T(4,128)(2,1)} %concatenate.86) | copy-start | bytes 2359300
  14.5 9.8 %copy-start.31 = (u32[128]{0:T(128)S(1)}, u32[128]{0:T(128)}, u32[]{:S(2)}) copy-start(u32[128]{0:T(128)} %constant.95) | copy-start | bytes 1540
  14.5 11.1 %copy-start.30 = (s32[1,12]{1,0:T(1,128)S(1)}, s32[1,12]{1,0:T(1,128)}, u32[]{:S(2)}) copy-start(s32[1,12]{1,0:T(1,128)} %param.11) | copy-start | bytes 148
  14.5 35.5 %all-to-all-start.1 = ((bf16[32,12,4,384]{3,2,1,0:T(4,128)(2,1)}), bf16[32,12,4,384]{3,2,1,0:T(4,128)(2,1)}, u32[]{:S(2)}, u32[]{:S(2)}) async-start(bf16[32,12,4,384]{3,2,1,0:T(4,128)(2,1)} %copy.41), calls=%async_computation.1 | async-start | bytes 2359296 | tf_op jit(solution)/shard_map/all_to_all | solution.py:274
  49.2 4.2 %copy-start.29 = (s32[384]{0:T(512)}, s32[384]{0:T(512)S(1)}, u32[]{:S(2)}) copy-start(s32[384]{0:T(512)S(1)} %get-tuple-element.41.index_ref) | copy-start | bytes 4612
  53.3 30.5 %all-to-all-start.2 = ((bf16[32,16,4,384]{3,2,1,0:T(4,128)(2,1)}), bf16[32,16,4,384]{3,2,1,0:T(4,128)(2,1)}, u32[]{:S(2)}, u32[]{:S(2)}) async-start(bf16[32,16,4,384]{3,2,1,0:T(4,128)(2,1)} %bitcast.56), calls=%async_computation.2 | async-start | bytes 3145728 | tf_op jit(solution)/shard_map/all_to_all | solution.py:274
  61.0 3.0 %copy-start.25 = (bf16[1024,128]{1,0:T(8,128)(2,1)S(1)}, bf16[1024,128]{1,0:T(8,128)(2,1)}, u32[]{:S(2)}) copy-start(bf16[1024,128]{1,0:T(8,128)(2,1)} %get-tuple-element.14) | copy-start | bytes 786436
  61.0 3.0 %copy-start.26 = (bf16[1024,128]{1,0:T(8,128)(2,1)S(1)}, bf16[1024,128]{1,0:T(8,128)(2,1)}, u32[]{:S(2)}) copy-start(bf16[1024,128]{1,0:T(8,128)(2,1)} %get-tuple-element.43) | copy-start | bytes 786436
  65.0 0.9 copy-start.8
  66.7 63.8 %collective-permute-start = (bf16[256,384]{1,0:T(8,128)(2,1)}, bf16[256,384]{1,0:T(8,128)(2,1)}, u32[]{:S(2)}, u32[]{:S(2)}) collective-permute-start(bf16[256,384]{1,0:T(8,128)(2,1)} %get-tuple-element.9), channel_id=1, source_target_pairs={{0,4},{4,8},{8,12},{12,16},{16,20},{20,24},{24,28},{28,32},{32,36}... | collective-permute-start | bytes 589832 | tf_op jit(solution)/shard_map/ppermute | solution.py:255
  70.2 60.2 %collective-permute-start.1 = (bf16[256,384]{1,0:T(8,128)(2,1)}, bf16[256,384]{1,0:T(8,128)(2,1)}, u32[]{:S(2)}, u32[]{:S(2)}) collective-permute-start(bf16[256,384]{1,0:T(8,128)(2,1)} %get-tuple-element.8), channel_id=1, source_target_pairs={{4,0},{8,4},{12,8},{16,12},{20,16},{24,20},{28,24},{32,28},{36,32}... | collective-permute-start | bytes 589832 | tf_op jit(solution)/shard_map/ppermute | solution.py:255
  72.2 3.5 %copy-start.9 = (bf16[1536,256]{1,0:T(8,128)(2,1)S(1)}, bf16[1536,256]{1,0:T(8,128)(2,1)}, u32[]{:S(2)}) copy-start(bf16[1536,256]{1,0:T(8,128)(2,1)} %copy-done.8) | copy-start | bytes 2359300
  83.8 33.5 %all-to-all-start = ((bf16[4,256,512]{2,1,0:T(8,128)(2,1)}), bf16[4,256,512]{2,1,0:T(8,128)(2,1)}, u32[]{:S(2)}, u32[]{:S(2)}) async-start(bf16[4,256,512]{2,1,0:T(8,128)(2,1)} %bitcast.59), calls=%async_computation | async-start | bytes 2097152 | tf_op jit(solution)/shard_map/all_to_all | solution.py:274
  117.4 39.1 %all-to-all-start.3 = ((bf16[32,16,4,384]{3,2,1,0:T(4,128)(2,1)}), bf16[32,16,4,384]{3,2,1,0:T(4,128)(2,1)}, u32[]{:S(2)}, u32[]{:S(2)}) async-start(bf16[32,16,4,384]{3,2,1,0:T(4,128)(2,1)} %bitcast.57), calls=%async_computation.3 | async-start | bytes 3145728 | tf_op jit(solution)/shard_map/all_to_all | solution.py:274
  156.4 21.8 %all-to-all-start.5 = ((bf16[32,32,384]{2,1,0:T(8,128)(2,1)}), bf16[32,32,384]{2,1,0:T(8,128)(2,1)}, u32[]{:S(2)}, u32[]{:S(2)}) async-start(bf16[32,32,384]{2,1,0:T(8,128)(2,1)} %fusion.7), calls=%async_computation.5 | async-start | bytes 1572864 | tf_op jit(solution)/shard_map/all_to_all | solution.py:274
  166.1 24.1 %collective-permute-start.3 = (bf16[1536,256]{1,0:T(8,128)(2,1)}, bf16[1536,256]{1,0:T(8,128)(2,1)}, u32[]{:S(2)}, u32[]{:S(2)}) collective-permute-start(bf16[1536,256]{1,0:T(8,128)(2,1)} %slice.158), channel_id=1, source_target_pairs={{0,3},{1,0},{2,1},{3,2},{4,7},{5,4},{6,5},{7,6},{8,11},{9,8},{10,9... | collective-permute-start | bytes 2359304 | tf_op jit(solution)/shard_map/ppermute | solution.py:260
  168.9 25.9 %collective-permute-start.2 = (bf16[1536,256]{1,0:T(8,128)(2,1)}, bf16[1536,256]{1,0:T(8,128)(2,1)}, u32[]{:S(2)}, u32[]{:S(2)}) collective-permute-start(bf16[1536,256]{1,0:T(8,128)(2,1)} %slice.158), channel_id=1, source_target_pairs={{0,1},{1,2},{2,3},{3,0},{4,5},{5,6},{6,7},{7,4},{8,9},{9,10},{10,1... | collective-permute-start | bytes 2359304 | tf_op jit(solution)/shard_map/ppermute | solution.py:260
  178.2 22.7 %all-to-all-start.4 = ((bf16[32,12,4,384]{3,2,1,0:T(4,128)(2,1)}), bf16[32,12,4,384]{3,2,1,0:T(4,128)(2,1)}, u32[]{:S(2)}, u32[]{:S(2)}) async-start(bf16[32,12,4,384]{3,2,1,0:T(4,128)(2,1)} %bitcast.58), calls=%async_computation.4 | async-start | bytes 2359296 | tf_op jit(solution)/shard_map/all_to_all | solution.py:274
  192.0 37.5 %collective-permute-start.5 = (bf16[768,256]{1,0:T(8,128)(2,1)}, bf16[768,256]{1,0:T(8,128)(2,1)S(1)}, u32[]{:S(2)}, u32[]{:S(2)}) collective-permute-start(bf16[768,256]{1,0:T(8,128)(2,1)} %slice.166), channel_id=1, source_target_pairs={{0,3},{1,0},{2,1},{3,2},{4,7},{5,4},{6,5},{7,6},{8,11},{9,8},{10,9... | collective-permute-start | bytes 1179656 | tf_op jit(solution)/shard_map/ppermute | solution.py:260
  196.6 32.9 %collective-permute-start.4 = (bf16[768,256]{1,0:T(8,128)(2,1)}, bf16[768,256]{1,0:T(8,128)(2,1)}, u32[]{:S(2)}, u32[]{:S(2)}) collective-permute-start(bf16[768,256]{1,0:T(8,128)(2,1)} %slice.165), channel_id=1, source_target_pairs={{0,1},{1,2},{2,3},{3,0},{4,5},{5,6},{6,7},{7,4},{8,9},{9,10},{10,1... | collective-permute-start | bytes 1179656 | tf_op jit(solution)/shard_map/ppermute | solution.py:260
  206.9 3.5 %copy-start.1 = (bf16[1536,384]{1,0:T(8,128)(2,1)S(1)}, bf16[1536,384]{1,0:T(8,128)(2,1)}, u32[]{:S(2)}) copy-start(bf16[1536,384]{1,0:T(8,128)(2,1)} %reshape.109) | copy-start | bytes 3538948
  219.5 18.7 %all-to-all-start.6 = ((bf16[32,32,384]{2,1,0:T(8,128)(2,1)}), bf16[32,32,384]{2,1,0:T(8,128)(2,1)}, u32[]{:S(2)}, u32[]{:S(2)}) async-start(bf16[32,32,384]{2,1,0:T(8,128)(2,1)} %fusion.8), calls=%async_computation.6 | async-start | bytes 1572864 | tf_op jit(solution)/shard_map/all_to_all | solution.py:274
  223.9 2.8 %copy-start.23 = (bf16[256,128]{1,0:T(8,128)(2,1)S(1)}, bf16[256,128]{1,0:T(8,128)(2,1)}, u32[]{:S(2)}) copy-start(bf16[256,128]{1,0:T(8,128)(2,1)} %get-tuple-element.22) | copy-start | bytes 196612
  223.9 2.8 %copy-start.24 = (bf16[256,128]{1,0:T(8,128)(2,1)S(1)}, bf16[256,128]{1,0:T(8,128)(2,1)}, u32[]{:S(2)}) copy-start(bf16[256,128]{1,0:T(8,128)(2,1)} %get-tuple-element.25) | copy-start | bytes 196612
  226.7 2.8 %copy-start.21 = (bf16[256,128]{1,0:T(8,128)(2,1)S(1)}, bf16[256,128]{1,0:T(8,128)(2,1)}, u32[]{:S(2)}) copy-start(bf16[256,128]{1,0:T(8,128)(2,1)} %get-tuple-element.30) | copy-start | bytes 196612
  226.7 2.8 %copy-start.22 = (bf16[256,128]{1,0:T(8,128)(2,1)S(1)}, bf16[256,128]{1,0:T(8,128)(2,1)}, u32[]{:S(2)}) copy-start(bf16[256,128]{1,0:T(8,128)(2,1)} %get-tuple-element.33) | copy-start | bytes 196612
  229.5 2.7 copy-start.2
  229.5 6.4 %copy-start.19 = (bf16[256,128]{1,0:T(8,128)(2,1)S(1)}, bf16[256,128]{1,0:T(8,128)(2,1)}, u32[]{:S(2)}) copy-start(bf16[256,128]{1,0:T(8,128)(2,1)} %get-tuple-element.19) | copy-start | bytes 196612
  229.5 6.4 %copy-start.20 = (bf16[256,128]{1,0:T(8,128)(2,1)S(1)}, bf16[256,128]{1,0:T(8,128)(2,1)}, u32[]{:S(2)}) copy-start(bf16[256,128]{1,0:T(8,128)(2,1)} %get-tuple-element.20) | copy-start | bytes 196612
  233.1 19.7 %collective-permute-start.7 = (bf16[1536,256]{1,0:T(8,128)(2,1)}, bf16[1536,256]{1,0:T(8,128)(2,1)}, u32[]{:S(2)}, u32[]{:S(2)}) collective-permute-start(bf16[1536,256]{1,0:T(8,128)(2,1)} %slice.169), channel_id=1, source_target_pairs={{0,3},{1,0},{2,1},{3,2},{4,7},{5,4},{6,5},{7,6},{8,11},{9,8},{10,9... | collective-permute-start | bytes 2359304 | tf_op jit(solution)/shard_map/ppermute | solution.py:260
  235.9 21.4 %collective-permute-start.6 = (bf16[1536,256]{1,0:T(8,128)(2,1)}, bf16[1536,256]{1,0:T(8,128)(2,1)}, u32[]{:S(2)}, u32[]{:S(2)}) collective-permute-start(bf16[1536,256]{1,0:T(8,128)(2,1)} %slice.169), channel_id=1, source_target_pairs={{0,1},{1,2},{2,3},{3,0},{4,5},{5,6},{6,7},{7,4},{8,9},{9,10},{10,1... | collective-permute-start | bytes 2359304 | tf_op jit(solution)/shard_map/ppermute | solution.py:260
  235.9 3.7 %copy-start.28 = (f32[32,128]{1,0:T(8,128)S(1)}, f32[32,128]{1,0:T(8,128)}, u32[]{:S(2)}) copy-start(f32[32,128]{1,0:T(8,128)} %get-tuple-element.36) | copy-start | bytes 49156
  235.9 4.3 %copy-start.27 = (f32[32,128]{1,0:T(8,128)S(1)}, f32[32,128]{1,0:T(8,128)}, u32[]{:S(2)}) copy-start(f32[32,128]{1,0:T(8,128)} %get-tuple-element.35) | copy-start | bytes 49156
  237.5 21.5 %copy-start.15 = (bf16[256,128]{1,0:T(8,128)(2,1)S(1)}, bf16[256,128]{1,0:T(8,128)(2,1)}, u32[]{:S(2)}) copy-start(bf16[256,128]{1,0:T(8,128)(2,1)} %get-tuple-element.23) | copy-start | bytes 196612
  237.5 21.5 %copy-start.16 = (bf16[256,128]{1,0:T(8,128)(2,1)S(1)}, bf16[256,128]{1,0:T(8,128)(2,1)}, u32[]{:S(2)}) copy-start(bf16[256,128]{1,0:T(8,128)(2,1)} %get-tuple-element.24) | copy-start | bytes 196612
  238.2 20.8 %copy-start.3 = (f32[1536,256]{1,0:T(8,128)S(1)}, f32[1536,256]{1,0:T(8,128)}, u32[]{:S(2)}) copy-start(f32[1536,256]{1,0:T(8,128)} %fusion.44) | copy-start | bytes 4718596
  253.8 10.8 %collective-permute-start.9 = (bf16[768,256]{1,0:T(8,128)(2,1)S(1)}, bf16[768,256]{1,0:T(8,128)(2,1)S(1)}, u32[]{:S(2)}, u32[]{:S(2)}) collective-permute-start(bf16[768,256]{1,0:T(8,128)(2,1)S(1)} %slice.177), channel_id=1, source_target_pairs={{0,3},{1,0},{2,1},{3,2},{4,7},{5,4},{6,5},{7,6},{8,11},{9,8},{10,9... | collective-permute-start | bytes 1179656 | tf_op jit(solution)/shard_map/ppermute | solution.py:260
  258.3 10.5 %collective-permute-start.8 = (bf16[768,256]{1,0:T(8,128)(2,1)S(1)}, bf16[768,256]{1,0:T(8,128)(2,1)S(1)}, u32[]{:S(2)}, u32[]{:S(2)}) collective-permute-start(bf16[768,256]{1,0:T(8,128)(2,1)S(1)} %slice.176), channel_id=1, source_target_pairs={{0,1},{1,2},{2,3},{3,0},{4,5},{5,6},{6,7},{7,4},{8,9},{9,10},{10,1... | collective-permute-start | bytes 1179656 | tf_op jit(solution)/shard_map/ppermute | solution.py:260
  259.0 9.8 %copy-start.17 = (bf16[256,128]{1,0:T(8,128)(2,1)S(1)}, bf16[256,128]{1,0:T(8,128)(2,1)}, u32[]{:S(2)}) copy-start(bf16[256,128]{1,0:T(8,128)(2,1)} %get-tuple-element.31) | copy-start | bytes 196612
  259.0 9.8 %copy-start.18 = (bf16[256,128]{1,0:T(8,128)(2,1)S(1)}, bf16[256,128]{1,0:T(8,128)(2,1)}, u32[]{:S(2)}) copy-start(bf16[256,128]{1,0:T(8,128)(2,1)} %get-tuple-element.32) | copy-start | bytes 196612
  260.6 8.6 %copy-start.13 = (bf16[256,128]{1,0:T(8,128)(2,1)S(1)}, bf16[256,128]{1,0:T(8,128)(2,1)}, u32[]{:S(2)}) copy-start(bf16[256,128]{1,0:T(8,128)(2,1)} %get-tuple-element.27) | copy-start | bytes 196612
  260.6 8.6 %copy-start.14 = (bf16[256,128]{1,0:T(8,128)(2,1)S(1)}, bf16[256,128]{1,0:T(8,128)(2,1)}, u32[]{:S(2)}) copy-start(bf16[256,128]{1,0:T(8,128)(2,1)} %get-tuple-element.28) | copy-start | bytes 196612
  268.8 2.2 copy-start.7
  269.2 1.7 copy-start.4
  269.2 2.2 copy-start.5
  269.3 2.7 copy-start.6
  269.3 2.7 copy-start.11
  269.3 2.6 copy-start.12

commit v2 on v1

--- a/solution.py
+++ b/solution.py
@@ -82,12 +82,13 @@
     )(index, chunks)
 
 
-def cluster_kernel(first_ref, data_ref, out_ref, key_buf, query_sums, key_sums, value_sums):
+def cluster_kernel(first_ref, chunk_ref, out_ref, data_ref, key_buf, query_sums, key_sums, value_sums, forward):
     key_sums[...] = jnp.zeros_like(key_sums)
     value_sums[...] = jnp.zeros_like(value_sums)
 
     def make_keys(slot, carry):
         rows = pl.ds(pl.multiple_of(slot * BLOCK, BLOCK), BLOCK)
+        data_ref[rows, :] = chunk_ref[:, slot].reshape(BLOCK, 3 * HEAD)
         floats = data_ref[rows, :HEAD].astype(jnp.float32)
         key_buf[rows, :] = (floats * unit_factor(floats)).astype(jnp.bfloat16)
         return carry
@@ -111,7 +112,7 @@
             allowed,
             self_spot,
         )
-        out_ref[rows, :HEAD] = outputs.astype(jnp.bfloat16)
+        forward[rows, :] = outputs.astype(jnp.bfloat16)
         query_sums[rows, :] = query_grads
         key_sums[span, :] += key_grads
         value_sums[span, :] += value_grads
@@ -140,15 +141,22 @@
         rows = pl.ds(pl.multiple_of(slot * BLOCK, BLOCK), BLOCK)
         floats = data_ref[rows, :HEAD].astype(jnp.float32)
         total = query_sums[rows, :] + chain(floats, key_sums[rows, :])
-        out_ref[rows, HEAD : 2 * HEAD] = total.astype(jnp.bfloat16)
-        out_ref[rows, 2 * HEAD :] = value_sums[rows, :].astype(jnp.bfloat16)
+        joined = jnp.concatenate(
+            [
+                forward[rows, :],
+                total.astype(jnp.bfloat16),
+                value_sums[rows, :].astype(jnp.bfloat16),
+            ],
+            axis=1,
+        )
+        out_ref[:, slot] = joined.reshape(chunk_ref.shape[0], chunk_ref.shape[2], 3 * HEAD)
         return carry
 
     lax.fori_loop(0, SLOTS, finish, 0)
 
 
 def cluster_attention(first, data):
-    rows = data.shape[0]
+    rows = SLOTS * BLOCK
     return pl.pallas_call(
         cluster_kernel,
         out_shape=jax.ShapeDtypeStruct(data.shape, jnp.bfloat16),
@@ -158,10 +166,12 @@
         ],
         out_specs=pl.BlockSpec(memory_space=pltpu.VMEM),
         scratch_shapes=[
+            pltpu.VMEM((rows, 3 * HEAD), jnp.bfloat16),
             pltpu.VMEM((rows, HEAD), jnp.bfloat16),
             pltpu.VMEM((rows, HEAD), jnp.float32),
             pltpu.VMEM((rows, HEAD), jnp.float32),
             pltpu.VMEM((rows, HEAD), jnp.float32),
+            pltpu.VMEM((rows, HEAD), jnp.bfloat16),
         ],
         cost_estimate=pl.CostEstimate(
             flops=12 << 30, bytes_accessed=4 << 20, transcendentals=1 << 20
@@ -260,16 +270,6 @@
     return lax.ppermute(value, axis, [(i, (i + steps) % count) for i in range(count)])
 
 
-def ring_gather(value, axis):
-    half = value.shape[0] // 2
-    left = turned(value, axis, 1)
-    right = turned(value, axis, -1)
-    far_top = turned(left[:half], axis, 1)
-    far_low = turned(right[half:], axis, -1)
-    far = jnp.concatenate([far_top, far_low], axis=0)
-    return value, left, right, far
-
-
 def exchange(value, axis):
     return lax.all_to_all(value, axis, split_axis=0, concat_axis=0, tiled=True)
 
@@ -294,6 +294,314 @@
     return target, picked, first
 
 
+def project_kernel(tokens_ref, shared_ref, value_ref, cotangent_ref, output_ref, out_ref):
+    tokens = tokens_ref[...]
+    joined = jnp.concatenate(
+        [
+            contract(tokens, shared_ref[...], 1, 0),
+            contract(tokens, value_ref[...], 1, 0),
+            contract(cotangent_ref[...], output_ref[...], 1, 1),
+        ],
+        axis=1,
+    ).astype(jnp.bfloat16)
+    if len(out_ref.shape) == 2:
+        out_ref[...] = joined
+        return
+    for slot in range(out_ref.shape[1]):
+        out_ref[:, slot] = joined[slot * BLOCK : (slot + 1) * BLOCK].reshape(
+            out_ref.shape[0], out_ref.shape[2], 3 * HEAD
+        )
+
+
+def project(tokens, shared_weight, value_weight, cotangent, output_weight, head, parts):
+    token_count, width = tokens.shape
+    if parts:
+        piece = BLOCK // parts
+        shape = (parts, token_count // BLOCK, piece, 3 * HEAD)
+        spec = pl.BlockSpec((parts, TILE // BLOCK, piece, 3 * HEAD), lambda i: (0, i, 0, 0))
+    else:
+        shape = (token_count, 3 * HEAD)
+        spec = pl.BlockSpec((TILE, 3 * HEAD), lambda i: (i, 0))
+    rows = pl.BlockSpec((TILE, width), lambda i: (i, 0))
+    columns = pl.BlockSpec((width, HEAD), lambda i: (0, head))
+    return pl.pallas_call(
+        project_kernel,
+        grid=(token_count // TILE,),
+        out_shape=jax.ShapeDtypeStruct(shape, jnp.bfloat16),
+        in_specs=[rows, columns, columns, rows, pl.BlockSpec((HEAD, width), lambda i: (head, 0))],
+        out_specs=spec,
+        cost_estimate=pl.CostEstimate(
+            flops=6 * token_count * width * HEAD, bytes_accessed=8 << 20, transcendentals=0
+        ),
+        name="project",
+    )(tokens, shared_weight, value_weight, cotangent, output_weight)
+
+
+def weight_terms(turned_rows, tokens_ref, cotangent_ref, scale, store):
+    def step(part, carry):
+        span = pl.ds(pl.multiple_of(part * TILE, TILE), TILE)
+        terms = jnp.concatenate(
+            [
+                contract(turned_rows[HEAD:, :], tokens_ref[:, span], 1, 0),
+                contract(turned_rows[:HEAD, :], cotangent_ref[:, span], 1, 0),
+            ],
+            axis=0,
+        )
+        store(part, (terms * scale).T.astype(jnp.bfloat16))
+        return carry
+
+    lax.fori_loop(0, tokens_ref.shape[1] // TILE, step, 0)
+
+
+def local_terms_kernel(scale, rows_ref, tokens_ref, cotangent_ref, out_ref, turned_rows):
+    turned_rows[...] = rows_ref[...].T
+
+    def store(part, terms):
+        out_ref[pl.ds(pl.multiple_of(part * TILE, TILE), TILE), :] = terms
+
+    weight_terms(turned_rows, tokens_ref, cotangent_ref, scale, store)
+
+
+def local_terms(rows, tokens, cotangent, scale):
+    count, width = tokens.shape
+    return pl.pallas_call(
+        functools.partial(local_terms_kernel, scale),
+        out_shape=jax.ShapeDtypeStruct((width, 3 * HEAD), jnp.bfloat16),
+        in_specs=[pl.BlockSpec(memory_space=pltpu.VMEM)] * 3,
+        out_specs=pl.BlockSpec(memory_space=pltpu.VMEM),
+        scratch_shapes=[pltpu.VMEM((3 * HEAD, count), jnp.bfloat16)],
+        cost_estimate=pl.CostEstimate(
+            flops=6 * count * width * HEAD, bytes_accessed=8 << 20, transcendentals=0
+        ),
+        name="local_terms",
+    )(rows, tokens, cotangent)
+
+
+MESH = pl.DeviceIdType.MESH
+
+
+def final_kernel(
+    seq_count,
+    wide_count,
+    scale,
+    home,
+    tokens_hbm,
+    cotangent_hbm,
+    local_ref,
+    part_ref,
+    columns,
+    token_out,
+    shared_out,
+    value_out,
+    output_out,
+    tokens_buf,
+    cotangent_buf,
+    rows_buf,
+    turned_rows,
+    from_left,
+    from_right,
+    from_far,
+    total,
+    pieces,
+    arrived,
+    load_sem,
+    send_sem,
+    recv_sem,
+    piece_send,
+    piece_recv,
+):
+    me = lax.axis_index("seq")
+    here = lax.axis_index("wide")
+    right = lax.rem(here + 1, wide_count)
+    left = lax.rem(here + wide_count - 1, wide_count)
+    far = lax.rem(here + 2, wide_count)
+    chunks, slots, piece = home.shape[:3]
+    half = chunks // 2
+    tops = pl.ds(0, half)
+    lows = pl.ds(half, half)
+    grads = pl.ds(HEAD, 2 * HEAD)
+
+    load_tokens = pltpu.make_async_copy(tokens_hbm, tokens_buf, load_sem.at[0])
+    load_cotangent = pltpu.make_async_copy(cotangent_hbm, cotangent_buf, load_sem.at[1])
+    load_tokens.start()
+    load_cotangent.start()
+
+    barrier = pltpu.get_barrier_semaphore()
+    for side in (left, right):
+        pl.semaphore_signal(barrier, inc=1, device_id={"wide": side}, device_id_type=MESH)
+
+    def greet(step, carry):
+        peer = lax.rem(me + step, seq_count)
+        pl.semaphore_signal(barrier, inc=1, device_id={"seq": peer}, device_id_type=MESH)
+        return carry
+
+    lax.fori_loop(1, seq_count, greet, 0)
+    pl.semaphore_wait(barrier, seq_count + 1)
+
+    def sending(source, target, number, side):
+        return pltpu.make_async_remote_copy(
+            src_ref=source,
+            dst_ref=target,
+            send_sem=send_sem.at[number],
+            recv_sem=recv_sem.at[number],
+            device_id={"wide": side},
+            device_id_type=MESH,
+        )
+
+    right_top = sending(home.at[tops, :, :, grads], from_left.at[tops], 0, right)
+    right_low = sending(home.at[lows, :, :, grads], from_left.at[lows], 1, right)
+    left_top = sending(home.at[tops, :, :, grads], from_right.at[tops], 2, left)
+    left_low = sending(home.at[lows, :, :, grads], from_right.at[lows], 3, left)
+    onward_top = sending(from_left.at[tops], from_far.at[tops], 4, right)
+    onward_low = sending(from_right.at[lows], from_far.at[lows], 5, left)
+    right_top.start()
+    left_low.start()
+    right_low.start()
+    left_top.start()
+
+    def merge(slot, carry):
+        span = pl.ds(pl.multiple_of(slot * BLOCK, BLOCK), BLOCK)
+        rows = home[:, slot].reshape(BLOCK, 3 * HEAD)
+        rows_buf[span, :] = rows
+        turned_rows[:, span] = rows.T
+        return carry
+
+    lax.fori_loop(0, slots, merge, 0)
+    load_tokens.wait()
+    load_cotangent.wait()
+    share = home.shape[0]
+    rows_each = pieces.shape[1]
+    per_part = TILE // rows_each
+
+    def store(part, terms):
+        pieces[pl.ds(part * per_part, per_part), :, 3 * HEAD :] = terms.reshape(
+            per_part, rows_each, 3 * HEAD
+        )
+
+    pieces[:, :, : 3 * HEAD] = local_ref[...]
+    weight_terms(turned_rows, tokens_buf, cotangent_buf, scale, store)
+
+    def piece_copy(peer, slot):
+        return pltpu.make_async_remote_copy(
+            src_ref=pieces.at[peer],
+            dst_ref=arrived.at[slot],
+            send_sem=piece_send.at[peer],
+            recv_sem=piece_recv.at[slot],
+            device_id={"seq": peer},
+            device_id_type=MESH,
+        )
+
+    def send_piece(step, carry):
+        piece_copy(lax.rem(me + step, seq_count), me).start()
+        return carry
+
+    lax.fori_loop(1, seq_count, send_piece, 0)
+
+    def add_terms(source, owner, first, last):
+        weights = columns[owner]
+
+        def step(slot, carry):
+            span = pl.ds(pl.multiple_of(slot * BLOCK, BLOCK), BLOCK)
+            rows = source(slot, span)
+            base = part_ref[span, :] if first else total[span, :]
+            value = base + contract(rows, weights, 1, 1)
+            if last:
+                token_out[span, :] = value.astype(jnp.bfloat16)
+            else:
+                total[span, :] = value
+            return carry
+
+        lax.fori_loop(0, slots, step, 0)
+
+    def merged(buffer):
+        return lambda slot, span: buffer[:, slot].reshape(BLOCK, 2 * HEAD)
+
+    right_top.wait_recv()
+    onward_top.start()
+    left_low.wait_recv()
+    onward_low.start()
+    add_terms(lambda slot, span: rows_buf[span, HEAD:], here, True, False)
+    right_low.wait_recv()
+    add_terms(merged(from_left), left, False, False)
+    left_top.wait_recv()
+    add_terms(merged(from_right), right, False, False)
+    onward_top.wait_recv()
+    onward_low.wait_recv()
+    add_terms(merged(from_far), far, False, True)
+
+    def take(step, sums):
+        peer = lax.rem(me + step, seq_count)
+        piece_copy(peer, peer).wait_recv()
+        return sums + arrived[peer].astype(jnp.float32)
+
+    sums = lax.fori_loop(1, seq_count, take, pieces[me].astype(jnp.float32))
+
+    def paired(number):
+        low = number * HEAD
+        return jnp.concatenate(
+            [sums[:, low : low + HEAD], sums[:, 3 * HEAD + low : 4 * HEAD + low]], axis=1
+        )
+
+    shared_out[...] = paired(0)
+    value_out[...] = paired(1)
+    output_out[...] = paired(2)
+
+    for copy in (right_top, right_low, left_top, left_low, onward_top, onward_low):
+        copy.wait_send()
+
+    def drain(step, carry):
+        peer = lax.rem(me + step, seq_count)
+        piece_copy(peer, me).wait_send()
+        return carry
+
+    lax.fori_loop(1, seq_count, drain, 0)
+
+
+def final_step(home, tokens, cotangent, local_part_terms, part, columns, scale):
+    count, width = tokens.shape
+    seq_count = lax.axis_size("seq")
+    wide_count = lax.axis_size("wide")
+    each = width // seq_count
+    out_width = width // wide_count
+    chunk = home.shape[:3] + (2 * HEAD,)
+    vmem = pl.BlockSpec(memory_space=pltpu.VMEM)
+    anywhere = pl.BlockSpec(memory_space=pl.ANY)
+    small = jax.ShapeDtypeStruct((each, 2 * HEAD), jnp.float32)
+    return pl.pallas_call(
+        functools.partial(final_kernel, seq_count, wide_count, scale),
+        out_shape=(
+            jax.ShapeDtypeStruct((count, out_width), jnp.bfloat16),
+            small,
+            small,
+            small,
+        ),
+        in_specs=[vmem, anywhere, anywhere, vmem, vmem, vmem],
+        out_specs=(vmem,) * 4,
+        scratch_shapes=[
+            pltpu.VMEM((count, width), jnp.bfloat16),
+            pltpu.VMEM((count, width), jnp.bfloat16),
+            pltpu.VMEM((count, 3 * HEAD), jnp.bfloat16),
+            pltpu.VMEM((3 * HEAD, count), jnp.bfloat16),
+            pltpu.VMEM(chunk, jnp.bfloat16),
+            pltpu.VMEM(chunk, jnp.bfloat16),
+            pltpu.VMEM(chunk, jnp.bfloat16),
+            pltpu.VMEM((count, out_width), jnp.float32),
+            pltpu.VMEM((seq_count, each, 6 * HEAD), jnp.bfloat16),
+            pltpu.VMEM((seq_count, each, 6 * HEAD), jnp.bfloat16),
+            pltpu.SemaphoreType.DMA((2,)),
+            pltpu.SemaphoreType.DMA((6,)),
+            pltpu.SemaphoreType.DMA((6,)),
+            pltpu.SemaphoreType.DMA((seq_count,)),
+            pltpu.SemaphoreType.DMA((seq_count,)),
+        ],
+        compiler_params=pltpu.CompilerParams(collective_id=0, has_side_effects=True),
+        cost_estimate=pl.CostEstimate(
+            flops=30 << 30, bytes_accessed=16 << 20, transcendentals=0
+        ),
+        name="final_step",
+    )(home, tokens, cotangent, local_part_terms, part, columns)
+
+
 def on_device(tokens, shared_weight, value_weight, output_weight, cotangent, block_clusters):
     seq_count = lax.axis_size("seq")
     wide_count = lax.axis_size("wide")
@@ -302,82 +610,57 @@
     token_count, width = tokens.shape
     block_count = token_count // BLOCK
     piece = BLOCK // seq_count
-
-    routed_pair = jnp.concatenate([shared_weight[:, HEAD:], value_weight[:, HEAD:]], axis=1)
-    routed = jnp.concatenate(
-        [contract(tokens, routed_pair, 1, 0), contract(cotangent, output_weight[HEAD:], 1, 1)],
-        axis=1,
-    ).astype(jnp.bfloat16)
-    leaving = routed.reshape(block_count, seq_count, piece, 3 * HEAD).transpose(1, 0, 2, 3)
-    labels = lax.all_gather(block_clusters[0], "seq", axis=0, tiled=True)
+    grad_scale = 1.0 / math.sqrt(seq_count * token_count)
+    ends = (tokens, shared_weight, value_weight, cotangent, output_weight)
+
+    leaving = project(*ends, 1, seq_count)
+    middle = exchange(leaving, "seq").reshape(seq_count * block_count, piece, 3 * HEAD)
+    spread = jnp.broadcast_to(block_clusters[None], (seq_count, 1, block_count))
+    labels = exchange(spread, "seq").reshape(seq_count * block_count)
     target, picked, first = route(labels, seq_count, block_count)
-    middle = exchange(leaving, "seq").reshape(seq_count * block_count, piece, 3 * HEAD)
-    sent = gather_chunks(picked, middle, seq_count * SLOTS)
-    arrived = exchange(sent.reshape(seq_count, SLOTS, piece, 3 * HEAD), "seq")
-    held = arrived.transpose(1, 0, 2, 3).reshape(SLOTS * BLOCK, 3 * HEAD)
-    own_first = lax.dynamic_slice_in_dim(first, position * SLOTS, SLOTS, 0)
-    results = cluster_attention(own_first, held)
-    turned_back = results.reshape(SLOTS, seq_count, piece, 3 * HEAD).transpose(1, 0, 2, 3)
-    middle_back = exchange(turned_back, "seq").reshape(seq_count * SLOTS, piece, 3 * HEAD)
-    homeward = gather_chunks(target, middle_back, seq_count * block_count)
-    home = exchange(homeward.reshape(seq_count, block_count, piece, 3 * HEAD), "seq")
-    routed_all = home.transpose(1, 0, 2, 3).reshape(token_count, 3 * HEAD)
-
-    local_pair = jnp.concatenate([shared_weight[:, :HEAD], value_weight[:, :HEAD]], axis=1)
-    local = jnp.concatenate(
-        [contract(tokens, local_pair, 1, 0), contract(cotangent, output_weight[:HEAD], 1, 1)],
-        axis=1,
-    ).astype(jnp.bfloat16)
+
+    local = project(*ends, 0, 0)
     before = shifted(local[token_count - WINDOW :], "seq", 1)
     after = shifted(local[:WINDOW], "seq", -1)
     place = jnp.stack([position, (position == seq_count - 1).astype(jnp.int32)])
+    weights = jnp.concatenate(
+        [shared_weight[:, :HEAD], value_weight[:, :HEAD], shared_weight[:, HEAD:], value_weight[:, HEAD:]],
+        axis=1,
+    )
+    columns = exchange(weights.reshape(wide_count, width // wide_count, 4 * HEAD), "wide")
+
+    sent = gather_chunks(picked, middle, seq_count * SLOTS)
+    sent, local = lax.optimization_barrier((sent, local))
+    arrived = exchange(sent.reshape(seq_count, SLOTS, piece, 3 * HEAD), "seq")
     local_all = band_attention(place, local, before, after)
 
-    weights = jnp.concatenate([shared_weight, value_weight], axis=1)
-    pieces = weights.reshape(wide_count, width // wide_count, weights.shape[1])
-    columns = exchange(pieces, "wide")
-
-    def input_part(grads, offset):
-        total = None
-        for steps, part in zip((0, 1, -1, 2), ring_gather(grads, "wide")):
-            owner = (here - steps) % wide_count
-            rows = lax.dynamic_slice_in_dim(columns, owner, 1, 0)[0]
-            rows = jnp.concatenate(
-                [rows[:, offset : offset + HEAD], rows[:, 2 * HEAD + offset : 3 * HEAD + offset]],
-                axis=1,
-            )
-            term = contract(part, rows, 1, 1)
-            total = term if total is None else total + term
-        return total
-
-    grad_scale = 1.0 / math.sqrt(seq_count * token_count)
-
-    def weight_part(rows):
-        terms = jnp.concatenate(
-            [contract(tokens, rows[:, HEAD:], 0, 0), contract(cotangent, rows[:, :HEAD], 0, 0)],
-            axis=1,
-        )
-        terms = (terms * grad_scale).astype(jnp.bfloat16)
-        terms = exchange(terms.reshape(seq_count, width // seq_count, 3 * HEAD), "seq")
-        return jnp.sum(terms.astype(jnp.float32), axis=0)
-
-    local_weights = weight_part(local_all)
-    routed_weights = weight_part(routed_all)
-    token_grads = (
-        input_part(local_all[:, HEAD:], 0) + input_part(routed_all[:, HEAD:], HEAD)
-    ).astype(jnp.bfloat16)
-
-    def paired(low, high):
-        return jnp.concatenate(
-            [local_weights[:, low:high], routed_weights[:, low:high]], axis=1
-        )
-
-    return (
-        token_grads,
-        paired(0, HEAD),
-        paired(HEAD, 2 * HEAD),
-        paired(2 * HEAD, 3 * HEAD).T,
+    own_first = lax.dynamic_slice_in_dim(first, position * SLOTS, SLOTS, 0)
+    results = cluster_attention(own_first, arrived)
+    results, local_all = lax.optimization_barrier((results, local_all))
+    middle_back = exchange(results, "seq").reshape(seq_count * SLOTS, piece, 3 * HEAD)
+    local_grads = local_all[:, HEAD:]
+    local_sides = [turned(local_grads, "wide", steps) for steps in (1, -1, 2)]
+    terms = local_terms(local_all, tokens, cotangent, grad_scale)
+    homeward = gather_chunks(target, middle_back, seq_count * block_count)
+    home = exchange(homeward.reshape(seq_count, block_count, piece, 3 * HEAD), "seq")
+
+    part = None
+    for steps, grads in zip((0, 1, -1, 2), [local_grads] + local_sides):
+        owner = (here - steps) % wide_count
+        rows = lax.dynamic_slice_in_dim(columns, owner, 1, 0)[0, :, : 2 * HEAD]
+        term = contract(grads, rows, 1, 1)
+        part = term if part is None else part + term
+
+    token_grads, shared_grads, value_grads, output_grads = final_step(
+        home,
+        tokens,
+        cotangent,
+        terms.reshape(seq_count, width // seq_count, 3 * HEAD),
+        part,
+        columns[:, :, 2 * HEAD :],
+        grad_scale,
     )
+    return token_grads, shared_grads, value_grads, output_grads.T
 
 
 def solution(mesh):

time: 276 us -> 218 us (0.79)
  Pallas kernels: 33.5 us -> 93 us
  local copies, waits for them, and re-layouts: 57.9 us -> 16.2 us
  matrix products: 35.6 us -> 6.86 us
  blocking collectives: 22.6 us -> 0 us
  starting transfers between devices: 68.8 us -> 53.8 us
  other arithmetic: 16.6 us -> 3.98 us
  waiting for transfers between devices: 36.4 us -> 42.2 us
    pallas_call x0 -> x4, Pallas kernels: none -> 59 us  [the longest x1 37.9 us: final_step(): pl.pallas_call(functools.partial(final_kernel, seq_count, wide_count, sca...]
    dot_general x16 -> x4, matrix products: 35.6 us -> 6.86 us  [contract(): lax.dot_general(left_side, right_side, (((left_dim,), (right_dim,)), ((),...]
    all_to_all x7 -> x6, waiting for transfers between devices: 16.2 us -> 42.2 us  [exchange(): return lax.all_to_all(value, axis, split_axis=0, concat_axis=0, tiled=True)]
    all_gather x1 -> x0, blocking collectives: 22.6 us -> none  [on_device(): labels = lax.all_gather(block_clusters[0], 'seq', axis=0, tiled=True)]
    ppermute x8 -> x3, waiting for transfers between devices: 20.1 us -> 0.01 us  [turned(): lax.ppermute(value, axis, [(i, (i + steps) % count) for i in range(count)])]
    reshape x4 -> x0, local copies, waits for them, and re-layouts: 14.1 us -> none  [the longest x2 7.24 us: on_device(): results.reshape(SLOTS, seq_count, piece, 3 * HEAD).transpose(1, 0, 2, 3)]
    dot_general x5 -> x0, local copies, waits for them, and re-layouts: 11.5 us -> none  [contract(): lax.dot_general(left_side, right_side, (((left_dim,), (right_dim,)), ((),...]
    slice x12 -> x3, local copies, waits for them, and re-layouts: 14.9 us -> 3.9 us  [the longest x1 1.89 us: on_device(): columns[:, :, 2 * HEAD:]]
  transfers between devices with their start and end apart: 17 -> 11, of which waited for: 7 -> 4; matrix products, arithmetic and copies ran while one was open for 33% -> 7% of each run, Pallas kernels for 11% -> 25%
where the time goes in v2:
time: 218 us; the launch traced here: 217 us
  Pallas kernels  93 us (43%)
  starting transfers between devices  53.8 us (25%)
  waiting for transfers between devices  42.2 us (19%)
  local copies, waits for them, and re-layouts  16.2 us (7%)
  matrix products  6.86 us (3%)
  other arithmetic  3.98 us (2%)
    all_to_all x6, starting transfers between devices, exchange(): return lax.all_to_all(value, axis, split_axis=0, concat_axis=0, tiled=True)  42.4 us
    all_to_all x6, waiting for transfers between devices, exchange(): return lax.all_to_all(value, axis, split_axis=0, concat_axis=0, tiled=True)  42.2 us
    pallas_call x1, Pallas kernels, final_step(): pl.pallas_call(functools.partial(final_kernel, seq_count, wide_count, sca...  37.9 us
    pallas_call x1, Pallas kernels, cluster_attention(): pl.pallas_call(cluster_kernel, out_shape=jax.ShapeDtypeStruct(data.shape,...  15.3 us
    pallas_call x2, Pallas kernels, project(): pl.pallas_call(project_kernel, grid=(token_count // TILE,), out_shape=jax...  14.4 us
    pallas_call x1, Pallas kernels, band_attention(): pl.pallas_call(band_kernel, out_shape=jax.ShapeDtypeStruct(data.shape, jn...  12.3 us
    unnamed x30, local copies, waits for them, and re-layouts  9.63 us
    dot_general x4, matrix products, contract(): lax.dot_general(left_side, right_side, (((left_dim,), (right_dim,)), ((),...  6.86 us
  transfers between devices with their start and end apart: 11, of which 4 were waited for; matrix products, arithmetic and copies ran while one was open for 7% of the time, Pallas kernels for 25%

profile of v2, /device:TPU:1, one launch (start us, length us, event | category | flops | bytes accessed | tf_op | source)
XLA Modules:
  0.0 216.8 jit_solution(14936798897540255212)
XLA Ops:
  0.6 1.3 broadcast_in_dim.50
  1.9 9.6 %all-to-all-start = ((s32[32,1,12]{2,1,0:T(1,128)}), s32[32,1,12]{2,1,0:T(1,128)S(1)}, u32[]{:S(2)}, u32[]{:S(2)}) async-start(s32[32,1,12]{2,1,0:T(1,128)} %broadcast_in_dim.50), calls=%async_computation | async-start | bytes 32768 | tf_op jit(solution)/shard_map/all_to_all | solution.py:274
  11.5 0.0 copy-start.2
  11.5 0.0 copy-start.3
  11.5 7.2 %project.3.data_ref = bf16[1536,384]{1,0:T(8,128)(2,1)} custom-call(bf16[1536,1024]{1,0:T(8,128)(2,1)} %tokens_hbm.1, bf16[1024,256]{1,0:T(8,128)(2,1)} %shared_ref.3, bf16[1024,256]{1,0:T(8,128)(2,1)} %value_ref.3, bf16[1536,1024]{1,0:T(8,128)(2,1)} %cotangent_hbm.1, bf16[256,1024]{1,0:T(8,128)(2,1)} %output_ref.3), custom_call_target="tpu_custom_call" | custom-call | flops 1207959552 | bytes 8388608 | tf_op jit(solution)/shard_map/project/pallas_call | solution.py:327
  18.7 1.1 fusion.12
  19.8 3.5 %collective-permute-start = (bf16[256,384]{1,0:T(8,128)(2,1)S(1)}, bf16[256,384]{1,0:T(8,128)(2,1)S(1)}, u32[]{:S(2)}, u32[]{:S(2)}) collective-permute-start(bf16[256,384]{1,0:T(8,128)(2,1)S(1)} %get-tuple-element.25), channel_id=1, source_target_pairs={{0,4},{4,8},{8,12},{12,16},{16,20},{20,24},{24,28},{28,32},{32,36}... | collective-permute-start | bytes 589832 | tf_op jit(solution)/shard_map/ppermute | solution.py:265
  23.3 1.9 collective-permute-start.1
  25.2 0.0 copy-done.2
  25.3 0.0 copy-done.3
  25.3 0.2 fusion.13
  25.5 1.1 pad_maximum_fusion
  26.6 7.2 %project.2 = bf16[32,12,4,384]{3,2,1,0:T(4,128)(2,1)} custom-call(bf16[1536,1024]{1,0:T(8,128)(2,1)} %tokens_hbm.1, bf16[1024,256]{1,0:T(8,128)(2,1)} %shared_ref.3, bf16[1024,256]{1,0:T(8,128)(2,1)} %value_ref.3, bf16[1536,1024]{1,0:T(8,128)(2,1)} %cotangent_hbm.1, bf16[256,1024]{1,0:T(8,128)(2,1)} %output_ref.3), custom_call_target="tpu_custom_call" | custom-call | flops 1207959552 | bytes 8388608 | tf_op jit(solution)/shard_map/project/pallas_call | solution.py:327
  33.7 0.0 all-to-all-done
  33.7 7.5 %all-to-all-start.1 = ((bf16[32,12,4,384]{3,2,1,0:T(4,128)(2,1)}), bf16[32,12,4,384]{3,2,1,0:T(4,128)(2,1)S(1)}, u32[]{:S(2)}, u32[]{:S(2)}) async-start(bf16[32,12,4,384]{3,2,1,0:T(4,128)(2,1)} %project.2), calls=%async_computation.1 | async-start | bytes 2359296 | tf_op jit(solution)/shard_map/all_to_all | solution.py:274
  41.2 0.5 broadcast.150
  41.7 0.7 reduce.3
  42.4 0.1 eq.51
  42.5 0.3 convert_reduce_fusion
  42.8 0.2 convert_reduce_fusion.1
  43.1 0.2 select_reduce_fusion.2
  43.4 0.0 copy-start.10
  43.4 0.8 select_reduce_fusion
  44.2 15.4 %all-to-all-done.1 = bf16[32,12,4,384]{3,2,1,0:T(4,128)(2,1)S(1)} async-done(((bf16[32,12,4,384]{3,2,1,0:T(4,128)(2,1)}), bf16[32,12,4,384]{3,2,1,0:T(4,128)(2,1)S(1)}, u32[]{:S(2)}, u32[]{:S(2)}) %all-to-all-start.1) | async-done | bytes 1179680 | tf_op jit(solution)/shard_map/all_to_all | solution.py:274
  59.6 1.0 copy-done.4
  60.6 3.3 %gather_chunks.2 = bf16[512,4,384]{2,1,0:T(4,128)(2,1)} custom-call(s32[512]{0:T(512)} %get-tuple-element.20.index_ref, bf16[384,4,384]{2,1,0:T(4,128)(2,1)} %bitcast.27), custom_call_target="tpu_custom_call" | custom-call | bytes 4194304 | tf_op jit(solution)/shard_map/gather_chunks/pallas_call | solution.py:72
  63.9 3.9 %all-to-all-start.2 = ((bf16[32,16,4,384]{3,2,1,0:T(4,128)(2,1)}), bf16[32,16,4,384]{3,2,1,0:T(4,128)(2,1)S(1)}, u32[]{:S(2)}, u32[]{:S(2)}) async-start(bf16[32,16,4,384]{3,2,1,0:T(4,128)(2,1)} %bitcast.26), calls=%async_computation.2 | async-start | bytes 3145728 | tf_op jit(solution)/shard_map/all_to_all | solution.py:274
  67.8 0.6 pad_add_fusion.place_ref
  68.4 0.6 dynamic_slice.15.first_ref
  69.0 0.0 collective-permute-done.before_ref
  69.0 0.0 collective-permute-done.1.after_ref
  69.0 0.7 copy-done.11
  69.7 0.7 copy-done.12
  70.3 12.3 %band_attention.1.rows_ref = bf16[1536,384]{1,0:T(8,128)(2,1)} custom-call(s32[2]{0:T(128)} %pad_add_fusion.place_ref, bf16[1536,384]{1,0:T(8,128)(2,1)} %project.3.data_ref, bf16[256,384]{1,0:T(8,128)(2,1)} %copy-done.11, bf16[256,384]{1,0:T(8,128)(2,1)} %copy-done.12), custom_call_target="tpu_custom_call" | custom-call | flops 12884901888 | bytes 4194304 | tf_op jit(solution)/shard_map/band_attention/pallas_call | solution.py:243
  82.6 7.9 %all-to-all-done.2.chunk_ref = bf16[32,16,4,384]{3,2,1,0:T(4,128)(2,1)S(1)} async-done(((bf16[32,16,4,384]{3,2,1,0:T(4,128)(2,1)}), bf16[32,16,4,384]{3,2,1,0:T(4,128)(2,1)S(1)}, u32[]{:S(2)}, u32[]{:S(2)}) %all-to-all-start.2) | async-done | bytes 1572896 | tf_op jit(solution)/shard_map/all_to_all | solution.py:274
  90.5 1.1 copy-done.6
  91.6 4.0 %all-to-all-start.5 = ((bf16[4,256,512]{2,1,0:T(8,128)(2,1)}), bf16[4,256,512]{2,1,0:T(8,128)(2,1)S(1)}, u32[]{:S(2)}, u32[]{:S(2)}) async-start(bf16[4,256,512]{2,1,0:T(8,128)(2,1)} %bitcast.8), calls=%async_computation.5 | async-start | bytes 2097152 | tf_op jit(solution)/shard_map/all_to_all | solution.py:274
  95.6 15.3 %cluster_attention.1 = bf16[32,16,4,384]{3,2,1,0:T(4,128)(2,1)} custom-call(s32[16]{0:T(128)} %dynamic_slice.15.first_ref, bf16[32,16,4,384]{3,2,1,0:T(4,128)(2,1)} %copy-done.6), custom_call_target="tpu_custom_call" | custom-call | flops 12884901888 | bytes 4194304 | tf_op jit(solution)/shard_map/cluster_attention/pallas_call | solution.py:160
  111.0 0.0 all-to-all-done.5
  111.0 1.0 copy-done.5
  111.9 12.7 %all-to-all-start.3 = ((bf16[32,16,4,384]{3,2,1,0:T(4,128)(2,1)}), bf16[32,16,4,384]{3,2,1,0:T(4,128)(2,1)S(1)}, u32[]{:S(2)}, u32[]{:S(2)}) async-start(bf16[32,16,4,384]{3,2,1,0:T(4,128)(2,1)} %cluster_attention.1), calls=%async_computation.3 | async-start | bytes 3145728 | tf_op jit(solution)/shard_map/all_to_all | solution.py:274
  124.6 0.9 slice.38
  125.6 3.2 %collective-permute-start.4 = (bf16[1536,256]{1,0:T(8,128)(2,1)}, bf16[1536,256]{1,0:T(8,128)(2,1)}, u32[]{:S(2)}, u32[]{:S(2)}) collective-permute-start(bf16[1536,256]{1,0:T(8,128)(2,1)} %slice.38), channel_id=1, source_target_pairs={{0,2},{1,3},{2,0},{3,1},{4,6},{5,7},{6,4},{7,5},{8,10},{9,11},{10,... | collective-permute-start | bytes 2359304 | tf_op jit(solution)/shard_map/ppermute | solution.py:270
  128.8 0.3 collective-permute-start.2
  129.1 1.9 slice.50.columns
  131.0 2.4 %collective-permute-start.3 = (bf16[1536,256]{1,0:T(8,128)(2,1)}, bf16[1536,256]{1,0:T(8,128)(2,1)}, u32[]{:S(2)}, u32[]{:S(2)}) collective-permute-start(bf16[1536,256]{1,0:T(8,128)(2,1)} %slice.38), channel_id=1, source_target_pairs={{0,3},{1,0},{2,1},{3,2},{4,7},{5,4},{6,5},{7,6},{8,11},{9,8},{10,9... | collective-permute-start | bytes 2359304 | tf_op jit(solution)/shard_map/ppermute | solution.py:270
  133.4 14.0 %all-to-all-done.3 = bf16[32,16,4,384]{3,2,1,0:T(4,128)(2,1)S(1)} async-done(((bf16[32,16,4,384]{3,2,1,0:T(4,128)(2,1)}), bf16[32,16,4,384]{3,2,1,0:T(4,128)(2,1)S(1)}, u32[]{:S(2)}, u32[]{:S(2)}) %all-to-all-start.3) | async-done | bytes 1572896 | tf_op jit(solution)/shard_map/all_to_all | solution.py:274
  147.4 1.2 copy-done.1
  148.5 3.1 %gather_chunks.3 = bf16[384,4,384]{2,1,0:T(4,128)(2,1)} custom-call(s32[384]{0:T(512)} %copy-done.10, bf16[512,4,384]{2,1,0:T(4,128)(2,1)} %bitcast.25), custom_call_target="tpu_custom_call" | custom-call | bytes 4194304 | tf_op jit(solution)/shard_map/gather_chunks/pallas_call | solution.py:72
  151.7 4.8 %all-to-all-start.4 = ((bf16[32,12,4,384]{3,2,1,0:T(4,128)(2,1)}), bf16[32,12,4,384]{3,2,1,0:T(4,128)(2,1)}, u32[]{:S(2)}, u32[]{:S(2)}) async-start(bf16[32,12,4,384]{3,2,1,0:T(4,128)(2,1)} %bitcast.28), calls=%async_computation.4 | async-start | bytes 2359296 | tf_op jit(solution)/shard_map/all_to_all | solution.py:274
  156.5 1.3 fusion.3
  157.8 6.7 %local_terms.1 = bf16[1024,384]{1,0:T(8,128)(2,1)} custom-call(bf16[1536,384]{1,0:T(8,128)(2,1)} %band_attention.1.rows_ref, bf16[1536,1024]{1,0:T(8,128)(2,1)} %tokens_hbm.1, bf16[1536,1024]{1,0:T(8,128)(2,1)} %cotangent_hbm.1), custom_call_target="tpu_custom_call" | custom-call | flops 1207959552 | bytes 8388608 | tf_op jit(solution)/shard_map/local_terms/pallas_call | solution.py:367
  164.5 0.0 collective-permute-done.4
  164.5 1.5 fusion.2
  166.0 0.0 collective-permute-done.2
  166.0 1.3 convolution_add_fusion.1
  167.4 0.0 collective-permute-done.3
  167.4 2.7 %fusion.part_ref = f32[1536,256]{1,0:T(8,128)} fusion(f32[1536,256]{1,0:T(8,128)S(1)} %fusion.2, f32[1536,256]{1,0:T(8,128)S(1)} %convolution_add_fusion.1, bf16[1536,256]{1,0:T(8,128)(2,1)} %collective-permute-done.3, bf16[4,256,512]{2,1,0:T(8,128)(2,1)} %copy-done.5, s32[]{:T(128)S(6)} %select_n.86), kind=kOutput, calls=%fused_computation.1 | convolution fusion | flops 202113024 | bytes 5636100 | tf_op jit(solution)/shard_map/dot_general | solution.py:23
  170.1 4.9 %all-to-all-done.4.home = bf16[32,12,4,384]{3,2,1,0:T(4,128)(2,1)} async-done(((bf16[32,12,4,384]{3,2,1,0:T(4,128)(2,1)}), bf16[32,12,4,384]{3,2,1,0:T(4,128)(2,1)}, u32[]{:S(2)}, u32[]{:S(2)}) %all-to-all-start.4) | async-done | bytes 1179680 | tf_op jit(solution)/shard_map/all_to_all | solution.py:274
  175.0 37.9 %final_step.1 = (bf16[1536,256]{1,0:T(8,128)(2,1)}, f32[32,256]{1,0:T(8,128)}, f32[32,256]{1,0:T(8,128)}, f32[32,256]{1,0:T(8,128)}) custom-call(bf16[32,12,4,384]{3,2,1,0:T(4,128)(2,1)} %all-to-all-done.4.home, bf16[1536,1024]{1,0:T(8,128)(2,1)} %tokens_hbm.1, bf16[1536,1024]{1,0:T(8,128)(2,1)} %cotangent_hbm.1, bf16[32,32,384]{2,1,0:T(8,128)(2,1)} %bitcast.29, ...), custom_call_target="tpu_custom_call" | custom-call | flops 32212254720 | bytes 16777216 | tf_op jit(solution)/shard_map/final_step/pallas_call | solution.py:570
  212.9 2.1 copy.14
  215.0 0.6 copy.15
  215.6 0.6 copy.16
  216.2 0.6 copy.17
  (19 shorter events, 0.1 us)
Async XLA Ops:
  1.9 31.8 %all-to-all-start = ((s32[32,1,12]{2,1,0:T(1,128)}), s32[32,1,12]{2,1,0:T(1,128)S(1)}, u32[]{:S(2)}, u32[]{:S(2)}) async-start(s32[32,1,12]{2,1,0:T(1,128)} %broadcast_in_dim.50), calls=%async_computation | async-start | bytes 32768 | tf_op jit(solution)/shard_map/all_to_all | solution.py:274
  11.5 13.8 %copy-start.2 = (bf16[1024,256]{1,0:T(8,128)(2,1)S(1)}, bf16[1024,256]{1,0:T(8,128)(2,1)}, u32[]{:S(2)}) copy-start(bf16[1024,256]{1,0:T(8,128)(2,1)} %shared_ref.3) | copy-start | bytes 1572868
  11.5 13.8 %copy-start.3 = (bf16[1024,256]{1,0:T(8,128)(2,1)S(1)}, bf16[1024,256]{1,0:T(8,128)(2,1)}, u32[]{:S(2)}) copy-start(bf16[1024,256]{1,0:T(8,128)(2,1)} %value_ref.3) | copy-start | bytes 1572868
  19.8 49.2 %collective-permute-start = (bf16[256,384]{1,0:T(8,128)(2,1)S(1)}, bf16[256,384]{1,0:T(8,128)(2,1)S(1)}, u32[]{:S(2)}, u32[]{:S(2)}) collective-permute-start(bf16[256,384]{1,0:T(8,128)(2,1)S(1)} %get-tuple-element.25), channel_id=1, source_target_pairs={{0,4},{4,8},{8,12},{12,16},{16,20},{20,24},{24,28},{28,32},{32,36}... | collective-permute-start | bytes 589832 | tf_op jit(solution)/shard_map/ppermute | solution.py:265
  23.3 45.7 %collective-permute-start.1 = (bf16[256,384]{1,0:T(8,128)(2,1)S(1)}, bf16[256,384]{1,0:T(8,128)(2,1)S(1)}, u32[]{:S(2)}, u32[]{:S(2)}) collective-permute-start(bf16[256,384]{1,0:T(8,128)(2,1)S(1)} %get-tuple-element.24), channel_id=1, source_target_pairs={{4,0},{8,4},{12,8},{16,12},{20,16},{24,20},{28,24},{32,28},{36,32}... | collective-permute-start | bytes 589832 | tf_op jit(solution)/shard_map/ppermute | solution.py:265
  33.7 25.9 %all-to-all-start.1 = ((bf16[32,12,4,384]{3,2,1,0:T(4,128)(2,1)}), bf16[32,12,4,384]{3,2,1,0:T(4,128)(2,1)S(1)}, u32[]{:S(2)}, u32[]{:S(2)}) async-start(bf16[32,12,4,384]{3,2,1,0:T(4,128)(2,1)} %project.2), calls=%async_computation.1 | async-start | bytes 2359296 | tf_op jit(solution)/shard_map/all_to_all | solution.py:274
  43.4 20.6 %copy-start.10 = (s32[384]{0:T(512)}, s32[384]{0:T(512)S(1)}, u32[]{:S(2)}) copy-start(s32[384]{0:T(512)S(1)} %get-tuple-element.31.index_ref) | copy-start | bytes 4612
  59.6 1.0 copy-start.4
  63.9 26.5 %all-to-all-start.2 = ((bf16[32,16,4,384]{3,2,1,0:T(4,128)(2,1)}), bf16[32,16,4,384]{3,2,1,0:T(4,128)(2,1)S(1)}, u32[]{:S(2)}, u32[]{:S(2)}) async-start(bf16[32,16,4,384]{3,2,1,0:T(4,128)(2,1)} %bitcast.26), calls=%async_computation.2 | async-start | bytes 3145728 | tf_op jit(solution)/shard_map/all_to_all | solution.py:274
  69.0 0.7 copy-start.11
  69.7 0.7 copy-start.12
  90.5 1.1 copy-start.6
  91.6 19.3 %all-to-all-start.5 = ((bf16[4,256,512]{2,1,0:T(8,128)(2,1)}), bf16[4,256,512]{2,1,0:T(8,128)(2,1)S(1)}, u32[]{:S(2)}, u32[]{:S(2)}) async-start(bf16[4,256,512]{2,1,0:T(8,128)(2,1)} %bitcast.8), calls=%async_computation.5 | async-start | bytes 2097152 | tf_op jit(solution)/shard_map/all_to_all | solution.py:274
  111.0 13.7 %copy-start = (bf16[1536,384]{1,0:T(8,128)(2,1)S(1)}, bf16[1536,384]{1,0:T(8,128)(2,1)}, u32[]{:S(2)}) copy-start(bf16[1536,384]{1,0:T(8,128)(2,1)} %band_attention.1.rows_ref) | copy-start | bytes 3538948
  111.0 1.0 copy-start.5
  111.9 35.4 %all-to-all-start.3 = ((bf16[32,16,4,384]{3,2,1,0:T(4,128)(2,1)}), bf16[32,16,4,384]{3,2,1,0:T(4,128)(2,1)S(1)}, u32[]{:S(2)}, u32[]{:S(2)}) async-start(bf16[32,16,4,384]{3,2,1,0:T(4,128)(2,1)} %cluster_attention.1), calls=%async_computation.3 | async-start | bytes 3145728 | tf_op jit(solution)/shard_map/all_to_all | solution.py:274
  125.6 38.9 %collective-permute-start.4 = (bf16[1536,256]{1,0:T(8,128)(2,1)}, bf16[1536,256]{1,0:T(8,128)(2,1)}, u32[]{:S(2)}, u32[]{:S(2)}) collective-permute-start(bf16[1536,256]{1,0:T(8,128)(2,1)} %slice.38), channel_id=1, source_target_pairs={{0,2},{1,3},{2,0},{3,1},{4,6},{5,7},{6,4},{7,5},{8,10},{9,11},{10,... | collective-permute-start | bytes 2359304 | tf_op jit(solution)/shard_map/ppermute | solution.py:270
  128.8 37.2 %collective-permute-start.2 = (bf16[1536,256]{1,0:T(8,128)(2,1)}, bf16[1536,256]{1,0:T(8,128)(2,1)S(1)}, u32[]{:S(2)}, u32[]{:S(2)}) collective-permute-start(bf16[1536,256]{1,0:T(8,128)(2,1)} %slice.38), channel_id=1, source_target_pairs={{0,1},{1,2},{2,3},{3,0},{4,5},{5,6},{6,7},{7,4},{8,9},{9,10},{10,1... | collective-permute-start | bytes 2359304 | tf_op jit(solution)/shard_map/ppermute | solution.py:270
  131.0 36.4 %collective-permute-start.3 = (bf16[1536,256]{1,0:T(8,128)(2,1)}, bf16[1536,256]{1,0:T(8,128)(2,1)}, u32[]{:S(2)}, u32[]{:S(2)}) collective-permute-start(bf16[1536,256]{1,0:T(8,128)(2,1)} %slice.38), channel_id=1, source_target_pairs={{0,3},{1,0},{2,1},{3,2},{4,7},{5,4},{6,5},{7,6},{8,11},{9,8},{10,9... | collective-permute-start | bytes 2359304 | tf_op jit(solution)/shard_map/ppermute | solution.py:270
  147.4 1.2 copy-start.1
  151.7 23.3 %all-to-all-start.4 = ((bf16[32,12,4,384]{3,2,1,0:T(4,128)(2,1)}), bf16[32,12,4,384]{3,2,1,0:T(4,128)(2,1)}, u32[]{:S(2)}, u32[]{:S(2)}) async-start(bf16[32,12,4,384]{3,2,1,0:T(4,128)(2,1)} %bitcast.28), calls=%async_computation.4 | async-start | bytes 2359296 | tf_op jit(solution)/shard_map/all_to_all | solution.py:274
  212.9 2.1 copy-start.9
  212.9 2.7 %copy-start.8 = (f32[32,256]{1,0:T(8,128)S(1)}, f32[32,256]{1,0:T(8,128)}, u32[]{:S(2)}) copy-start(f32[32,256]{1,0:T(8,128)} %get-tuple-element.40) | copy-start | bytes 98308
  212.9 3.3 %copy-start.7 = (f32[32,256]{1,0:T(8,128)S(1)}, f32[32,256]{1,0:T(8,128)}, u32[]{:S(2)}) copy-start(f32[32,256]{1,0:T(8,128)} %get-tuple-element.19) | copy-start | bytes 98308

commit v3 on v2

v3 whole, which is shorter than its diff:
```python
import functools
import math

import jax
import jax.numpy as jnp
from jax import lax
from jax.experimental import pallas as pl
from jax.experimental.pallas import tpu as pltpu
from jax.sharding import PartitionSpec as P

HEAD = 128
WINDOW = 256
BLOCK = 128
MOST = 8
SLOTS = 16

EPSILON = 1e-06
NEGATIVE = -1e30
TILE = 256
GROUP = 4
BAND_GROUP = 3


def contract(left_side, right_side, left_dim, right_dim):
    return lax.dot_general(
        left_side,
        right_side,
        (((left_dim,), (right_dim,)), ((), ())),
        preferred_element_type=jnp.float32,
    )


def unit_factor(floats):
    return lax.rsqrt(jnp.mean(floats * floats, axis=-1, keepdims=True) + EPSILON)


def chain(floats, key_grads):
    factor = unit_factor(floats)
    inner_sum = jnp.sum(floats * key_grads, axis=-1, keepdims=True)
    return factor * key_grads - factor**3 / HEAD * floats * inner_sum


SCALE = 1.0 / math.sqrt(HEAD)
POWER = SCALE * math.log2(math.e)


def attend(jobs):
    scores = [mask(contract(q, k, 1, 1)) for q, k, v, t, mask, unself in jobs]
    prob_grads = [contract(t, v, 1, 1) for q, k, v, t, mask, unself in jobs]
    highest = [jnp.max(s, axis=1, keepdims=True) for s in scores]
    weights = [jnp.exp2((s - h) * POWER) for s, h in zip(scores, highest)]
    shares = [1.0 / jnp.sum(w, axis=1, keepdims=True) for w in weights]
    halves = [(w * share).astype(jnp.bfloat16) for w, share in zip(weights, shares)]
    centres = [
        share * jnp.sum(w * g, axis=1, keepdims=True)
        for w, g, share in zip(weights, prob_grads, shares)
    ]
    score_halves = [
        job[5](w * (share * SCALE) * (g - c)).astype(jnp.bfloat16)
        for job, w, share, g, c in zip(jobs, weights, shares, prob_grads, centres)
    ]
    outputs = [contract(h, job[2], 1, 0) for h, job in zip(halves, jobs)]
    query_grads = [contract(h, job[1], 1, 0) for h, job in zip(score_halves, jobs)]
    value_grads = [contract(h, job[3], 0, 0) for h, job in zip(halves, jobs)]
    key_grads = [contract(h, job[0], 0, 0) for h, job in zip(score_halves, jobs)]
    return zip(outputs, query_grads, key_grads, value_grads)


def cluster_kernel(
    first_ref, chunk_ref, out_ref, data_ref, key_buf, query_sums, key_sums, value_sums, forward
):
    pad = (MOST - 1) * BLOCK
    key_sums[...] = jnp.zeros_like(key_sums)
    value_sums[...] = jnp.zeros_like(value_sums)
    data_ref[:pad, :] = jnp.zeros((pad, 3 * HEAD), jnp.bfloat16)
    key_buf[:pad, :] = jnp.zeros((pad, HEAD), jnp.bfloat16)

    def rows_of(slot):
        return pl.ds(pl.multiple_of((slot + MOST - 1) * BLOCK, BLOCK), BLOCK)

    def make_keys(slot, carry):
        rows = rows_of(slot)
        data = chunk_ref[:, slot].reshape(BLOCK, 3 * HEAD)
        data_ref[rows, :] = data
        floats = data[:, :HEAD].astype(jnp.float32)
        key_buf[rows, :] = (floats * unit_factor(floats)).astype(jnp.bfloat16)
        return carry

    lax.fori_loop(0, SLOTS, make_keys, 0, unroll=4)
    spot = lax.broadcasted_iota(jnp.int32, (BLOCK, BLOCK), 1)
    row = lax.broadcasted_iota(jnp.int32, (BLOCK, BLOCK), 0)

    def unself(grads):
        width = grads.shape[1]
        last = jnp.where(spot == row, 0.0, grads[:, width - BLOCK :])
        if width == BLOCK:
            return last
        return jnp.concatenate([grads[:, : width - BLOCK], last], axis=1)

    def visit(begin, counts, reach):
        width = reach * BLOCK
        jobs = []
        for number, count in enumerate(counts):
            rows = rows_of(begin + number)
            span = pl.ds(pl.multiple_of((begin + number + MOST - reach) * BLOCK, BLOCK), width)

            def mask(scores, count=count):
                last = jnp.where(
                    spot < row,
                    scores[:, width - BLOCK :],
                    jnp.where(spot == row, 0.0, NEGATIVE),
                )
                if reach == 1:
                    return last
                place = lax.broadcasted_iota(jnp.int32, (BLOCK, width - BLOCK), 1)
                least = (reach - count) * BLOCK
                rest = jnp.where(place >= least, scores[:, : width - BLOCK], NEGATIVE)
                return jnp.concatenate([rest, last], axis=1)

            jobs.append(
                (
                    data_ref[rows, :HEAD],
                    key_buf[span, :],
                    data_ref[span, HEAD : 2 * HEAD],
                    data_ref[rows, 2 * HEAD :],
                    mask,
                    unself,
                )
            )
        for number, (outputs, query_grads, key_grads, value_grads) in enumerate(attend(jobs)):
            rows = rows_of(begin + number)
            span = pl.ds(pl.multiple_of((begin + number + MOST - reach) * BLOCK, BLOCK), width)
            forward[rows, :] = outputs.astype(jnp.bfloat16)
            query_sums[rows, :] = query_grads
            key_sums[span, :] += key_grads
            value_sums[span, :] += value_grads

    def step(group, carry):
        begin = group * GROUP
        counts = []
        for number in range(GROUP):
            first = first_ref[begin + number]
            counts.append(jnp.where(first >= 0, begin + number - first + 1, 1))
        most = functools.reduce(jnp.maximum, counts)
        for low, reach in ((0, 1), (1, 2), (2, 4), (4, MOST)):

            @pl.when((most > low) & (most <= reach))
            def _(reach=reach):
                visit(begin, counts, reach)

        return carry

    lax.fori_loop(0, SLOTS // GROUP, step, 0)

    def finish(slot, carry):
        rows = rows_of(slot)
        floats = data_ref[rows, :HEAD].astype(jnp.float32)
        total = query_sums[rows, :] + chain(floats, key_sums[rows, :])
        joined = jnp.concatenate(
            [
                forward[rows, :],
                total.astype(jnp.bfloat16),
                value_sums[rows, :].astype(jnp.bfloat16),
            ],
            axis=1,
        )
        out_ref[:, slot] = joined.reshape(chunk_ref.shape[0], chunk_ref.shape[2], 3 * HEAD)
        return carry

    lax.fori_loop(0, SLOTS, finish, 0, unroll=4)


def cluster_attention(first, data):
    rows = (SLOTS + MOST - 1) * BLOCK
    return pl.pallas_call(
        cluster_kernel,
        out_shape=jax.ShapeDtypeStruct(data.shape, jnp.bfloat16),
        in_specs=[
            pl.BlockSpec(memory_space=pltpu.SMEM),
            pl.BlockSpec(memory_space=pltpu.VMEM),
        ],
        out_specs=pl.BlockSpec(memory_space=pltpu.VMEM),
        scratch_shapes=[
            pltpu.VMEM((rows, 3 * HEAD), jnp.bfloat16),
            pltpu.VMEM((rows, HEAD), jnp.bfloat16),
            pltpu.VMEM((rows, HEAD), jnp.float32),
            pltpu.VMEM((rows, HEAD), jnp.float32),
            pltpu.VMEM((rows, HEAD), jnp.float32),
            pltpu.VMEM((rows, HEAD), jnp.bfloat16),
        ],
        cost_estimate=pl.CostEstimate(
            flops=12 << 30, bytes_accessed=4 << 20, transcendentals=1 << 20
        ),
        name="cluster_attention",
    )(first, data)


def band_body(
    is_first, is_last, data_ref, before_ref, after_ref, out_ref, ext, key_buf, query_sums, key_sums, value_sums
):
    own = data_ref.shape[0]
    tiles = own // TILE
    ext[:WINDOW, :] = before_ref[...]
    ext[WINDOW : WINDOW + own, :] = data_ref[...]
    after = after_ref[...]
    ext[WINDOW + own :, :] = jnp.where(is_last, jnp.zeros_like(after), after)
    key_sums[...] = jnp.zeros_like(key_sums)
    value_sums[...] = jnp.zeros_like(value_sums)

    def make_keys(tile, carry):
        rows = pl.ds(pl.multiple_of(tile * TILE, TILE), TILE)
        floats = ext[rows, :HEAD].astype(jnp.float32)
        key_buf[rows, :] = (floats * unit_factor(floats)).astype(jnp.bfloat16)
        return carry

    lax.fori_loop(0, tiles + 2, make_keys, 0, unroll=4)
    spot = lax.broadcasted_iota(jnp.int32, (TILE, TILE), 1)
    row = lax.broadcasted_iota(jnp.int32, (TILE, TILE), 0)

    def unself(grads):
        last = jnp.where(spot == row, 0.0, grads[:, WINDOW:])
        return jnp.concatenate([grads[:, :WINDOW], last], axis=1)

    def mask(scores, tile):
        inside = spot >= row
        if tile == 0:
            inside = inside & (spot >= jnp.where(is_first, WINDOW, 0))
        first = jnp.where(inside, scores[:, :WINDOW], NEGATIVE)
        last = jnp.where(
            spot < row, scores[:, WINDOW:], jnp.where(spot == row, 0.0, NEGATIVE)
        )
        return jnp.concatenate([first, last], axis=1)

    for begin in range(0, tiles + 1, BAND_GROUP):
        group = range(begin, min(begin + BAND_GROUP, tiles + 1))
        jobs = []
        for tile in group:
            rows = pl.ds(tile * TILE + WINDOW, TILE)
            span = pl.ds(tile * TILE, TILE + WINDOW)
            jobs.append(
                (
                    ext[rows, :HEAD],
                    key_buf[span, :],
                    ext[span, HEAD : 2 * HEAD],
                    ext[rows, 2 * HEAD :],
                    functools.partial(mask, tile=tile),
                    unself,
                )
            )
        for tile, (outputs, query_grads, key_grads, value_grads) in zip(group, attend(jobs)):
            rows = pl.ds(tile * TILE + WINDOW, TILE)
            span = pl.ds(tile * TILE, TILE + WINDOW)
            query_sums[rows, :] = query_grads
            key_sums[span, :] += key_grads
            value_sums[span, :] += value_grads
            if tile < tiles:
                out_ref[pl.ds(tile * TILE, TILE), :HEAD] = outputs.astype(jnp.bfloat16)

    def finish(tile, carry):
        rows = pl.ds(pl.multiple_of(tile * TILE + WINDOW, TILE), TILE)
        into = pl.ds(pl.multiple_of(tile * TILE, TILE), TILE)
        floats = ext[rows, :HEAD].astype(jnp.float32)
        total = query_sums[rows, :] + chain(floats, key_sums[rows, :])
        out_ref[into, HEAD : 2 * HEAD] = total.astype(jnp.bfloat16)
        out_ref[into, 2 * HEAD :] = value_sums[rows, :].astype(jnp.bfloat16)
        return carry

    lax.fori_loop(0, tiles, finish, 0, unroll=3)


def route(labels, seq_count, per_device):
    order = jnp.arange(labels.shape[0], dtype=jnp.int32)
    same = labels[None, :] == labels[:, None]
    rank = jnp.sum(same & (order[None, :] < order[:, None]), axis=1).astype(jnp.int32)
    size = jnp.sum(same, axis=1).astype(jnp.int32)
    rating = size * 4096 - labels
    start = jnp.sum(rating[None, :] > rating[:, None], axis=1).astype(jnp.int32)
    owner = start // per_device
    base = jnp.min(
        jnp.where(owner[None, :] == owner[:, None], start[None, :], labels.shape[0]), axis=1
    ).astype(jnp.int32)
    target = owner * SLOTS + start + rank - base
    head = owner * SLOTS + start - base
    spots = jnp.arange(seq_count * SLOTS, dtype=jnp.int32)
    hits = target[None, :] == spots[:, None]
    picked = jnp.sum(jnp.where(hits, order[None, :], 0), axis=1).astype(jnp.int32)
    first = jnp.sum(jnp.where(hits, head[None, :] % SLOTS + 1, 0), axis=1).astype(jnp.int32) - 1
    return target, picked, first


def project_tile(tokens, cotangent, shared_ref, value_ref, output_ref):
    return jnp.concatenate(
        [
            contract(tokens, shared_ref[...], 1, 0),
            contract(tokens, value_ref[...], 1, 0),
            contract(cotangent, output_ref[...], 1, 1),
        ],
        axis=1,
    ).astype(jnp.bfloat16)


def project_kernel(tokens_ref, shared_ref, value_ref, cotangent_ref, output_ref, out_ref):
    joined = project_tile(tokens_ref[...], cotangent_ref[...], shared_ref, value_ref, output_ref)
    for slot in range(out_ref.shape[1]):
        out_ref[:, slot] = joined[slot * BLOCK : (slot + 1) * BLOCK].reshape(
            out_ref.shape[0], out_ref.shape[2], 3 * HEAD
        )


def project(tokens, shared_weight, value_weight, cotangent, output_weight, parts):
    token_count, width = tokens.shape
    piece = BLOCK // parts
    rows = pl.BlockSpec((TILE, width), lambda i: (i, 0))
    columns = pl.BlockSpec((width, HEAD), lambda i: (0, 1))
    return pl.pallas_call(
        project_kernel,
        grid=(token_count // TILE,),
        out_shape=jax.ShapeDtypeStruct(
            (parts, token_count // BLOCK, piece, 3 * HEAD), jnp.bfloat16
        ),
        in_specs=[rows, columns, columns, rows, pl.BlockSpec((HEAD, width), lambda i: (1, 0))],
        out_specs=pl.BlockSpec((parts, TILE // BLOCK, piece, 3 * HEAD), lambda i: (0, i, 0, 0)),
        name="project",
    )(tokens, shared_weight, value_weight, cotangent, output_weight)


def weight_terms(turned_rows, tokens_ref, cotangent_ref, scale, store):
    def step(part, carry):
        span = pl.ds(pl.multiple_of(part * TILE, TILE), TILE)
        terms = jnp.concatenate(
            [
                contract(turned_rows[HEAD:, :], tokens_ref[:, span], 1, 0),
                contract(turned_rows[:HEAD, :], cotangent_ref[:, span], 1, 0),
            ],
            axis=0,
        )
        store(part, (terms * scale).T.astype(jnp.bfloat16))
        return carry

    lax.fori_loop(0, tokens_ref.shape[1] // TILE, step, 0)


MESH = pl.DeviceIdType.MESH


def remote(source, target, send_sem, recv_sem, axis, peer):
    return pltpu.make_async_remote_copy(
        src_ref=source,
        dst_ref=target,
        send_sem=send_sem,
        recv_sem=recv_sem,
        device_id={axis: peer},
        device_id_type=MESH,
    )


def greet(barrier, axis, me, count):
    def step(number, carry):
        peer = lax.rem(me + number, count)
        pl.semaphore_signal(barrier, inc=1, device_id={axis: peer}, device_id_type=MESH)
        return carry

    lax.fori_loop(1, count, step, 0)


def start_kernel(
    seq_count,
    wide_count,
    leaving,
    marks,
    tokens_hbm,
    cotangent_hbm,
    shared_ref,
    value_ref,
    output_ref,
    middle,
    labels,
    local,
    before,
    after,
    shared_rows,
    value_rows,
    tokens_buf,
    cotangent_buf,
    load_sem,
    send_sem,
    recv_sem,
):
    me = lax.axis_index("seq")
    here = lax.axis_index("wide")
    load_tokens = pltpu.make_async_copy(tokens_hbm, tokens_buf, load_sem.at[0])
    load_cotangent = pltpu.make_async_copy(cotangent_hbm, cotangent_buf, load_sem.at[1])
    load_tokens.start()
    load_cotangent.start()
    barrier = pltpu.get_barrier_semaphore()
    greet(barrier, "seq", me, seq_count)
    greet(barrier, "wide", here, wide_count)
    pl.semaphore_wait(barrier, seq_count + wide_count - 2)

    def send(step, carry):
        peer = lax.rem(me + step, seq_count)
        remote(leaving.at[peer], middle.at[me], send_sem.at[0], recv_sem.at[0], "seq", peer).start()
        return carry

    lax.fori_loop(1, seq_count, send, 0)
    own = pltpu.make_async_copy(leaving.at[me], middle.at[me], load_sem.at[2])
    own.start()

    def send_marks(step, carry):
        peer = lax.rem(me + step, seq_count)
        remote(marks, labels.at[me], send_sem.at[1], recv_sem.at[1], "seq", peer).start()
        return carry

    lax.fori_loop(1, seq_count, send_marks, 0)
    labels[me] = marks[...]
    each = shared_rows.shape[1]

    def rows_of(owner):
        return pl.ds(pl.multiple_of(owner * each, each), each)

    for step in range(1, wide_count):
        peer = lax.rem(here + step, wide_count)
        rows = rows_of(peer)
        remote(
            shared_ref.at[rows], shared_rows.at[here], send_sem.at[2], recv_sem.at[2], "wide", peer
        ).start()
        remote(
            value_ref.at[rows], value_rows.at[here], send_sem.at[3], recv_sem.at[3], "wide", peer
        ).start()
    shared_rows[here] = shared_ref[rows_of(here), :]
    value_rows[here] = value_ref[rows_of(here), :]

    load_tokens.wait()
    load_cotangent.wait()
    tiles = local.shape[0] // TILE

    def make(tile):
        rows = pl.ds(tile * TILE, TILE)
        local[rows, :] = project_tile(
            tokens_buf[rows, :],
            cotangent_buf[rows, :],
            shared_ref.at[:, :HEAD],
            value_ref.at[:, :HEAD],
            output_ref.at[:HEAD, :],
        )

    make(tiles - 1)
    make(0)
    make(1)
    following = lax.rem(me + 1, seq_count)
    previous = lax.rem(me + seq_count - 1, seq_count)
    low = pl.ds((tiles - 1) * TILE, TILE)
    onward = remote(local.at[low], before, send_sem.at[4], recv_sem.at[4], "seq", following)
    backward = remote(local.at[pl.ds(0, TILE)], after, send_sem.at[5], recv_sem.at[5], "seq", previous)
    onward.start()
    backward.start()
    for tile in range(2, tiles - 1):
        make(tile)

    own.wait()
    peers = seq_count - 1
    sides = wide_count - 1
    many = middle.at[pl.ds(0, peers)]
    marked = labels.at[pl.ds(0, peers)]
    few = shared_rows.at[pl.ds(0, sides)]
    fewer = value_rows.at[pl.ds(0, sides)]
    waits = (
        remote(many, many, send_sem.at[0], recv_sem.at[0], "seq", following),
        remote(marked, marked, send_sem.at[1], recv_sem.at[1], "seq", following),
        remote(few, few, send_sem.at[2], recv_sem.at[2], "seq", following),
        remote(fewer, fewer, send_sem.at[3], recv_sem.at[3], "seq", following),
        onward,
        backward,
    )
    for copy in waits:
        copy.wait_recv()
    for copy in waits:
        copy.wait_send()


def start_step(leaving, marks, tokens, cotangent, shared_weight, value_weight, output_weight):
    seq_count = lax.axis_size("seq")
    wide_count = lax.axis_size("wide")
    count, width = tokens.shape
    own_width = shared_weight.shape[1]
    vmem = pl.BlockSpec(memory_space=pltpu.VMEM)
    anywhere = pl.BlockSpec(memory_space=pl.ANY)
    half = jnp.bfloat16
    halo = jax.ShapeDtypeStruct((WINDOW, 3 * HEAD), half)
    rows = jax.ShapeDtypeStruct((wide_count, width // wide_count, own_width), half)
    return pl.pallas_call(
        functools.partial(start_kernel, seq_count, wide_count),
        out_shape=(
            jax.ShapeDtypeStruct(leaving.shape, half),
            jax.ShapeDtypeStruct((seq_count,) + marks.shape, jnp.int32),
            jax.ShapeDtypeStruct((count, 3 * HEAD), half),
            halo,
            halo,
            rows,
            rows,
        ),
        in_specs=[anywhere, vmem, anywhere, anywhere, vmem, vmem, vmem],
        out_specs=(vmem,) * 7,
        scratch_shapes=[
            pltpu.VMEM((count, width), half),
            pltpu.VMEM((count, width), half),
            pltpu.SemaphoreType.DMA((3,)),
            pltpu.SemaphoreType.DMA((6,)),
            pltpu.SemaphoreType.DMA((6,)),
        ],
        compiler_params=pltpu.CompilerParams(collective_id=0, has_side_effects=True),
        name="start_step",
    )(leaving, marks, tokens, cotangent, shared_weight, value_weight, output_weight)


LAG = 3


def gather_and_send(me, seq_count, index_ref, source, staged, landing, each, send_sem, recv_sem):
    def pick(peer, store):
        for number in range(each):
            store(number, source[index_ref[peer * each + number]])

    def send(step):
        peer = lax.rem(me + step, seq_count)
        remote(staged.at[peer], landing.at[me], send_sem, recv_sem(step), "seq", peer).start()

    def step(number, carry):
        peer = lax.rem(me + number, seq_count)

        def store(slot, value):
            staged[peer, slot] = value

        pick(peer, store)

        @pl.when(number > LAG)
        def _():
            send(number - LAG)

        return carry

    lax.fori_loop(1, seq_count, step, 0)

    def keep(slot, value):
        landing[me, slot] = value

    pick(me, keep)
    for number in range(seq_count - LAG, seq_count):
        send(number)


def middle_kernel(
    seq_count,
    picked,
    middle,
    local,
    before,
    after,
    arrived,
    local_all,
    staged,
    ext,
    key_buf,
    query_sums,
    key_sums,
    value_sums,
    send_sem,
    recv_sem,
):
    me = lax.axis_index("seq")
    barrier = pltpu.get_barrier_semaphore()
    greet(barrier, "seq", me, seq_count)
    pl.semaphore_wait(barrier, seq_count - 1)
    gather_and_send(
        me,
        seq_count,
        picked,
        middle,
        staged,
        arrived,
        SLOTS,
        send_sem.at[0],
        lambda step: recv_sem.at[0],
    )
    band_body(
        me == 0,
        me == seq_count - 1,
        local,
        before,
        after,
        local_all,
        ext,
        key_buf,
        query_sums,
        key_sums,
        value_sums,
    )
    many = arrived.at[pl.ds(0, seq_count - 1)]
    done = remote(many, many, send_sem.at[0], recv_sem.at[0], "seq", lax.rem(me + 1, seq_count))
    done.wait_recv()
    done.wait_send()


def middle_step(picked, middle, local, before, after):
    seq_count = lax.axis_size("seq")
    piece = middle.shape[1]
    count = local.shape[0]
    rows = count + 2 * WINDOW
    vmem = pl.BlockSpec(memory_space=pltpu.VMEM)
    half = jnp.bfloat16
    shape = (seq_count, SLOTS, piece, 3 * HEAD)
    return pl.pallas_call(
        functools.partial(middle_kernel, seq_count),
        out_shape=(
            jax.ShapeDtypeStruct(shape, half),
            jax.ShapeDtypeStruct((count, 3 * HEAD), half),
        ),
        in_specs=[pl.BlockSpec(memory_space=pltpu.SMEM)] + [vmem] * 4,
        out_specs=(vmem, vmem),
        scratch_shapes=[
            pltpu.VMEM(shape, half),
            pltpu.VMEM((rows, 3 * HEAD), half),
            pltpu.VMEM((rows, HEAD), half),
            pltpu.VMEM((rows, HEAD), jnp.float32),
            pltpu.VMEM((rows, HEAD), jnp.float32),
            pltpu.VMEM((rows, HEAD), jnp.float32),
            pltpu.SemaphoreType.DMA((1,)),
            pltpu.SemaphoreType.DMA((1,)),
        ],
        compiler_params=pltpu.CompilerParams(collective_id=1, has_side_effects=True),
        name="middle_step",
    )(picked, middle, local, before, after)


GROUPS = 4


def final_kernel(
    seq_count,
    wide_count,
    scale,
    target,
    results,
    tokens_hbm,
    cotangent_hbm,
    local,
    shared_rows,
    value_rows,
    token_out,
    shared_out,
    value_out,
    output_out,
    back,
    staged,
    home,
    tokens_buf,
    cotangent_buf,
    rows_buf,
    turned_rows,
    local_left,
    local_right,
    local_far,
    from_left,
    from_right,
    from_far,
    total,
    local_pieces,
    local_arrived,
    pieces,
    arrived,
    load_sem,
    side_send,
    side_recv,
    home_recv,
    ring_send,
    ring_recv,
    bulk_send,
    bulk_recv,
):
    me = lax.axis_index("seq")
    here = lax.axis_index("wide")
    right = lax.rem(here + 1, wide_count)
    left = lax.rem(here + wide_count - 1, wide_count)
    far = lax.rem(here + 2, wide_count)
    following = lax.rem(me + 1, seq_count)
    slots = home.shape[1]
    count = rows_buf.shape[0]
    peers = seq_count - 1
    grads = pl.ds(HEAD, 2 * HEAD)

    load_tokens = pltpu.make_async_copy(tokens_hbm, tokens_buf, load_sem.at[0])
    load_cotangent = pltpu.make_async_copy(cotangent_hbm, cotangent_buf, load_sem.at[1])
    load_tokens.start()
    load_cotangent.start()
    barrier = pltpu.get_barrier_semaphore()
    for side in (left, right):
        pl.semaphore_signal(barrier, inc=1, device_id={"wide": side}, device_id_type=MESH)
    greet(barrier, "seq", me, seq_count)
    pl.semaphore_wait(barrier, peers + 2)

    def send_back(step, carry):
        peer = lax.rem(me + step, seq_count)
        remote(
            results.at[peer],
            back.at[pl.ds(me * SLOTS, SLOTS)],
            bulk_send.at[0],
            bulk_recv.at[0],
            "seq",
            peer,
        ).start()
        return carry

    lax.fori_loop(1, seq_count, send_back, 0)

    tops = pl.ds(0, count // 2)
    lows = pl.ds(count // 2, count // 2)

    def side(source, target_ref, number, peer):
        return remote(source, target_ref, side_send.at[number], side_recv.at[number], "wide", peer)

    right_top = side(local.at[tops, grads], local_left.at[tops], 0, right)
    right_low = side(local.at[lows, grads], local_left.at[lows], 1, right)
    left_top = side(local.at[tops, grads], local_right.at[tops], 2, left)
    left_low = side(local.at[lows, grads], local_right.at[lows], 3, left)
    onward_top = side(local_left.at[tops], local_far.at[tops], 4, right)
    onward_low = side(local_right.at[lows], local_far.at[lows], 5, left)
    right_top.start()
    left_low.start()
    right_low.start()
    left_top.start()

    back[pl.ds(me * SLOTS, SLOTS)] = results[me]
    turned_rows[...] = local[...].T
    load_tokens.wait()
    load_cotangent.wait()
    rows_each = pieces.shape[1]
    per_part = TILE // rows_each

    def storing(buffer):
        def store(part, terms):
            buffer[pl.ds(part * per_part, per_part)] = terms.reshape(per_part, rows_each, 3 * HEAD)

        return store

    weight_terms(turned_rows, tokens_buf, cotangent_buf, scale, storing(local_pieces))
    right_top.wait_recv()
    onward_top.start()
    left_low.wait_recv()
    onward_low.start()

    all_back = back.at[pl.ds(0, peers * SLOTS)]
    back_done = remote(all_back, all_back, bulk_send.at[0], bulk_recv.at[0], "seq", following)
    back_done.wait_recv()

    group_size = seq_count // GROUPS

    def group_of(step):
        return step // group_size

    gather_and_send(
        me,
        seq_count,
        target,
        back,
        staged,
        home,
        slots,
        bulk_send.at[1],
        lambda step: home_recv.at[group_of(step)],
    )

    def piece_copy(buffer, landing, number, peer):
        return remote(
            buffer.at[peer], landing.at[me], bulk_send.at[number], bulk_recv.at[number], "seq", peer
        )

    def send_local(step, carry):
        piece_copy(local_pieces, local_arrived, 2, lax.rem(me + step, seq_count)).start()
        return carry

    lax.fori_loop(1, seq_count, send_local, 0)

    def add_terms(source, owner, head, first, last):
        columns = pl.ds(head * HEAD, HEAD)
        weights = jnp.concatenate(
            [shared_rows[owner, :, columns], value_rows[owner, :, columns]], axis=1
        )

        def step(slot, carry):
            span = pl.ds(pl.multiple_of(slot * BLOCK, BLOCK), BLOCK)
            value = contract(source(slot, span), weights, 1, 1)
            if not first:
                value = value + total[span, :]
            if last:
                token_out[span, :] = value.astype(jnp.bfloat16)
            else:
                total[span, :] = value
            return carry

        lax.fori_loop(0, slots, step, 0, unroll=2)

    add_terms(lambda slot, span: local[span, HEAD:], here, 0, True, False)
    right_low.wait_recv()
    add_terms(lambda slot, span: local_left[span, :], left, 0, False, False)
    left_top.wait_recv()
    add_terms(lambda slot, span: local_right[span, :], right, 0, False, False)
    onward_top.wait_recv()
    onward_low.wait_recv()
    add_terms(lambda slot, span: local_far[span, :], far, 0, False, False)

    def ring(number, group, source, target_ref, peer):
        spot = number * GROUPS + group
        return remote(source, target_ref, ring_send.at[spot], ring_recv.at[spot], "wide", peer)

    def ring_all(number, group, buffer, target_buffer, peer):
        def step(place, carry):
            chunk = lax.rem(me + seq_count - group * group_size - place, seq_count)
            if buffer.shape[3] == 2 * HEAD:
                source = buffer.at[chunk]
            else:
                source = buffer.at[chunk, :, :, grads]
            ring(number, group, source, target_buffer.at[chunk], peer).start()
            return carry

        lax.fori_loop(0, group_size, step, 0)

    def ring_done(number, group, buffer):
        whole = buffer.at[pl.ds(0, group_size)]
        return ring(number, group, whole, whole, right)

    def home_done(group):
        size = group_size - 1 if group == 0 else group_size
        whole = home.at[pl.ds(0, size)]
        return remote(whole, whole, bulk_send.at[1], home_recv.at[group], "seq", following)

    def forward(group):
        if group % 2 == 0:
            ring_done(0, group, from_left).wait_recv()
            ring_all(2, group, from_left, from_far, right)
        else:
            ring_done(1, group, from_right).wait_recv()
            ring_all(2, group, from_right, from_far, left)

    for group in range(GROUPS):
        home_done(group).wait_recv()
        ring_all(0, group, home, from_left, right)
        ring_all(1, group, home, from_right, left)

    def merge(slot, carry):
        span = pl.ds(pl.multiple_of(slot * BLOCK, BLOCK), BLOCK)
        rows = home[:, slot].reshape(BLOCK, 3 * HEAD)
        rows_buf[span, :] = rows
        turned_rows[:, span] = rows.T
        return carry

    lax.fori_loop(0, slots, merge, 0, unroll=2)
    forward(0)
    forward(1)
    weight_terms(turned_rows, tokens_buf, cotangent_buf, scale, storing(pieces))

    def send_piece(step, carry):
        piece_copy(pieces, arrived, 3, lax.rem(me + step, seq_count)).start()
        return carry

    lax.fori_loop(1, seq_count, send_piece, 0)
    forward(2)
    forward(3)

    def merged(buffer):
        return lambda slot, span: buffer[:, slot].reshape(BLOCK, 2 * HEAD)

    add_terms(lambda slot, span: rows_buf[span, HEAD:], here, 1, False, False)
    ring_done(0, 1, from_left).wait_recv()
    ring_done(0, 3, from_left).wait_recv()
    add_terms(merged(from_left), left, 1, False, False)
    ring_done(1, 0, from_right).wait_recv()
    ring_done(1, 2, from_right).wait_recv()
    add_terms(merged(from_right), right, 1, False, False)

    def sums_of(number, buffer, landing):
        whole = landing.at[pl.ds(0, peers)]
        done = remote(whole, whole, bulk_send.at[number], bulk_recv.at[number], "seq", following)
        done.wait_recv()

        def step(place, sums):
            return sums + landing[lax.rem(me + place, seq_count)].astype(jnp.float32)

        return lax.fori_loop(1, seq_count, step, buffer[me].astype(jnp.float32)), done

    local_sums, local_done = sums_of(2, local_pieces, local_arrived)
    for group in range(GROUPS):
        ring_done(2, group, from_far).wait_recv()
    add_terms(merged(from_far), far, 1, False, True)
    routed_sums, routed_done = sums_of(3, pieces, arrived)

    def paired(number):
        columns = slice(number * HEAD, (number + 1) * HEAD)
        return jnp.concatenate([local_sums[:, columns], routed_sums[:, columns]], axis=1)

    shared_out[...] = paired(0)
    value_out[...] = paired(1)
    output_out[...] = paired(2)

    for copy in (right_top, right_low, left_top, left_low, onward_top, onward_low):
        copy.wait_send()
    back_done.wait_send()
    whole_home = home.at[pl.ds(0, peers)]
    remote(whole_home, whole_home, bulk_send.at[1], bulk_recv.at[1], "seq", following).wait_send()
    local_done.wait_send()
    routed_done.wait_send()
    for number in range(3):
        for group in range(GROUPS):
            ring_done(number, group, from_far).wait_send()


def final_step(target, results, tokens, cotangent, local_all, shared_rows, value_rows, scale):
    count, width = tokens.shape
    seq_count = lax.axis_size("seq")
    wide_count = lax.axis_size("wide")
    each = width // seq_count
    out_width = width // wide_count
    slots = count // BLOCK
    piece = results.shape[2]
    half = jnp.bfloat16
    vmem = pl.BlockSpec(memory_space=pltpu.VMEM)
    anywhere = pl.BlockSpec(memory_space=pl.ANY)
    small = jax.ShapeDtypeStruct((each, 2 * HEAD), jnp.float32)
    full = pltpu.VMEM((seq_count, slots, piece, 3 * HEAD), half)
    chunk = pltpu.VMEM((seq_count, slots, piece, 2 * HEAD), half)
    flat = pltpu.VMEM((count, 2 * HEAD), half)
    terms = pltpu.VMEM((seq_count, each, 3 * HEAD), half)
    return pl.pallas_call(
        functools.partial(final_kernel, seq_count, wide_count, scale),
        out_shape=(jax.ShapeDtypeStruct((count, out_width), half), small, small, small),
        in_specs=[pl.BlockSpec(memory_space=pltpu.SMEM), vmem, anywhere, anywhere, vmem, vmem, vmem],
        out_specs=(vmem,) * 4,
        scratch_shapes=[
            pltpu.VMEM((seq_count * SLOTS, piece, 3 * HEAD), half),
            full,
            full,
            pltpu.VMEM((count, width), half),
            pltpu.VMEM((count, width), half),
            pltpu.VMEM((count, 3 * HEAD), half),
            pltpu.VMEM((3 * HEAD, count), half),
            flat,
            flat,
            flat,
            chunk,
            chunk,
            chunk,
            pltpu.VMEM((count, out_width), jnp.float32),
            terms,
            terms,
            terms,
            terms,
            pltpu.SemaphoreType.DMA((2,)),
            pltpu.SemaphoreType.DMA((6,)),
            pltpu.SemaphoreType.DMA((6,)),
            pltpu.SemaphoreType.DMA((GROUPS,)),
            pltpu.SemaphoreType.DMA((3 * GROUPS,)),
            pltpu.SemaphoreType.DMA((3 * GROUPS,)),
            pltpu.SemaphoreType.DMA((4,)),
            pltpu.SemaphoreType.DMA((4,)),
        ],
        compiler_params=pltpu.CompilerParams(collective_id=2, has_side_effects=True),
        name="final_step",
    )(target, results, tokens, cotangent, local_all, shared_rows, value_rows)


def on_device(tokens, shared_weight, value_weight, output_weight, cotangent, block_clusters):
    seq_count = lax.axis_size("seq")
    position = lax.axis_index("seq")
    token_count = tokens.shape[0]
    block_count = token_count // BLOCK
    piece = BLOCK // seq_count
    grad_scale = 1.0 / math.sqrt(seq_count * token_count)

    leaving = project(tokens, shared_weight, value_weight, cotangent, output_weight, seq_count)
    marks = jnp.pad(block_clusters, ((0, 7), (0, HEAD - block_count)))
    middle, labels, local, before, after, shared_rows, value_rows = start_step(
        leaving, marks, tokens, cotangent, shared_weight, value_weight, output_weight
    )
    labels = labels[:, 0, :block_count].reshape(seq_count * block_count)
    target, picked, first = route(labels, seq_count, block_count)
    middle = middle.reshape(seq_count * block_count, piece, 3 * HEAD)
    arrived, local_all = middle_step(picked, middle, local, before, after)
    own_first = lax.dynamic_slice_in_dim(first, position * SLOTS, SLOTS, 0)
    results = cluster_attention(own_first, arrived)
    token_grads, shared_grads, value_grads, output_grads = final_step(
        target, results, tokens, cotangent, local_all, shared_rows, value_rows, grad_scale
    )
    return token_grads, shared_grads, value_grads, output_grads.T


def solution(mesh):
    placed = (
        P("seq", None),
        P(None, "wide"),
        P(None, "wide"),
        P("wide", None),
        P("seq", None),
        P("wide", "seq"),
    )
    return jax.shard_map(
        on_device,
        mesh=mesh,
        in_specs=placed,
        out_specs=(P("seq", "wide"), P("seq", "wide"), P("seq", "wide"), P("wide", "seq")),
        check_vma=False,
    )
```

time: 218 us -> 167 us (0.77)
  Pallas kernels: 93 us -> 158 us
  starting transfers between devices: 53.8 us -> 0 us
  waiting for transfers between devices: 42.2 us -> 0 us
  local copies, waits for them, and re-layouts: 16.2 us -> 6.18 us
  matrix products: 6.86 us -> 0 us
  other arithmetic: 3.98 us -> 1.63 us
    all_to_all x6 -> x0, starting transfers between devices: 42.4 us -> none  [exchange(): return lax.all_to_all(value, axis, split_axis=0, concat_axis=0, tiled=True)]
    all_to_all x6 -> x0, waiting for transfers between devices: 42.2 us -> none  [exchange(): return lax.all_to_all(value, axis, split_axis=0, concat_axis=0, tiled=True)]
    pallas_call x1, Pallas kernels: 37.9 us -> 78.3 us  [final_step(): pl.pallas_call(functools.partial(final_kernel, seq_count, wide_count, sca...]
    pallas_call x4 -> x2, Pallas kernels: 25.4 us -> 62.4 us  [the longest x1 31.3 us: start_step(): pl.pallas_call(functools.partial(start_kernel, seq_count, wide_count), ou...]
    ppermute x5 -> x0, starting transfers between devices: 11.4 us -> none  [the longest x3 5.92 us: turned(): lax.ppermute(value, axis, [(i, (i + steps) % count) for i in range(count)])]
    pallas_call x2 -> x1, Pallas kernels: 14.4 us -> 7.17 us  [project(): pl.pallas_call(project_kernel, grid=(token_count // TILE,), out_shape=jax...]
    dot_general x4 -> x0, matrix products: 6.86 us -> none  [contract(): lax.dot_general(left_side, right_side, (((left_dim,), (right_dim,)), ((),...]
    unnamed x30 -> x14, local copies, waits for them, and re-layouts: 9.63 us -> 3.95 us
  transfers between devices with their start and end apart: 11 -> 0, of which waited for: 4 -> 0; matrix products, arithmetic and copies ran while one was open for 7% -> 0% of each run, Pallas kernels for 25% -> 0%
where the time goes in v3:
time: 167 us; the launch traced here: 166 us
  Pallas kernels  158 us (95%)
  local copies, waits for them, and re-layouts  6.18 us (4%)
    pallas_call x1, Pallas kernels, final_step(): pl.pallas_call(functools.partial(final_kernel, seq_count, wide_count, sca...  78.3 us
    pallas_call x1, Pallas kernels, start_step(): pl.pallas_call(functools.partial(start_kernel, seq_count, wide_count), ou...  31.3 us
    pallas_call x1, Pallas kernels, middle_step(): pl.pallas_call(functools.partial(middle_kernel, seq_count), out_shape=(ja...  31.1 us
    pallas_call x1, Pallas kernels, cluster_attention(): pl.pallas_call(cluster_kernel, out_shape=jax.ShapeDtypeStruct(data.shape,...  10 us
    pallas_call x1, Pallas kernels, project(): pl.pallas_call(project_kernel, grid=(token_count // TILE,), out_shape=jax...  7.17 us
    unnamed x14, local copies, waits for them, and re-layouts  3.95 us

profile of v3, /device:TPU:1, one launch (start us, length us, event | category | flops | bytes accessed | tf_op | source)
XLA Modules:
  0.0 166.5 jit_solution(4690352559840811415)
XLA Ops:
  0.6 0.0 copy-start.4
  0.6 7.2 %project.1.leaving = bf16[32,12,4,384]{3,2,1,0:T(4,128)(2,1)} custom-call(bf16[1536,1024]{1,0:T(8,128)(2,1)} %tokens_hbm.3, bf16[1024,256]{1,0:T(8,128)(2,1)} %shared_ref.3, bf16[1024,256]{1,0:T(8,128)(2,1)} %value_ref.3, bf16[1536,1024]{1,0:T(8,128)(2,1)} %cotangent_hbm.3, bf16[256,1024]{1,0:T(8,128)(2,1)} %output_ref.3), custom_call_target="tpu_custom_call" | custom-call | tf_op jit(solution)/shard_map/project/pallas_call | solution.py:315
  7.8 0.0 copy-done.4
  7.8 0.6 pad.4.marks
  8.4 31.3 %start_step.1 = (bf16[32,12,4,384]{3,2,1,0:T(4,128)(2,1)}, s32[32,8,128]{2,1,0:T(8,128)}, bf16[1536,384]{1,0:T(8,128)(2,1)}, bf16[256,384]{1,0:T(8,128)(2,1)}, b...) custom-call(bf16[32,12,4,384]{3,2,1,0:T(4,128)(2,1)} %project.1.leaving, ...), custom_call_target="tpu_custom_call" | custom-call | tf_op jit(solution)/shard_map/start_step/pallas_call | solution.py:491
  39.7 0.9 slice_reduce_fusion
  40.7 0.1 eq.21
  40.8 0.3 convert_reduce_fusion
  41.1 0.2 convert_reduce_fusion.1
  41.3 0.2 select_reduce_fusion.2
  41.6 0.0 copy-start.3
  41.6 0.8 select_reduce_fusion
  42.4 0.6 dynamic_slice.3.first_ref
  43.0 31.1 %middle_step.1 = (bf16[32,16,4,384]{3,2,1,0:T(4,128)(2,1)}, bf16[1536,384]{1,0:T(8,128)(2,1)}) custom-call(s32[512]{0:T(512)} %get-tuple-element.30.picked, bf16[384,4,384]{2,1,0:T(4,128)(2,1)} %bitcast.2, bf16[1536,384]{1,0:T(8,128)(2,1)} %get-tuple-element.19.local, bf16[256,384]{1,0:T(8,128)(2,1)} %get-tuple-element.20.before, ...), custom_call_target="tpu_custom_call" | custom-call | tf_op jit(solution)/shard_map/middle_step/pallas_call | solution.py:612
  74.1 10.0 %cluster_attention.1.results = bf16[32,16,4,384]{3,2,1,0:T(4,128)(2,1)} custom-call(s32[16]{0:T(128)} %dynamic_slice.3.first_ref, bf16[32,16,4,384]{3,2,1,0:T(4,128)(2,1)} %get-tuple-element.22.chunk_ref), custom_call_target="tpu_custom_call" | custom-call | flops 12884901888 | bytes 4194304 | tf_op jit(solution)/shard_map/cluster_attention/pallas_call | solution.py:175
  84.2 0.0 copy-done.3
  84.2 78.3 %final_step.1 = (bf16[1536,256]{1,0:T(8,128)(2,1)}, f32[32,256]{1,0:T(8,128)}, f32[32,256]{1,0:T(8,128)}, f32[32,256]{1,0:T(8,128)}) custom-call(s32[384]{0:T(512)} %copy-done.3, bf16[32,16,4,384]{3,2,1,0:T(4,128)(2,1)} %cluster_attention.1.results, bf16[1536,1024]{1,0:T(8,128)(2,1)} %tokens_hbm.3, bf16[1536,1024]{1,0:T(8,128)(2,1)} %cotangent_hbm.3, ...), custom_call_target="tpu_custom_call" | custom-call | tf_op jit(solution)/shard_map/final_step/pallas_call | solution.py:932
  162.5 0.0 copy-start.2
  162.5 0.0 copy-start.1
  162.5 0.0 copy-start
  162.6 2.1 %copy.14 = bf16[1536,256]{1,0:T(8,128)(2,1)} copy(bf16[1536,256]{1,0:T(8,128)(2,1)} %get-tuple-element.40) | data formatting | bytes 1572864
  164.6 0.0 copy-done.2
  164.6 0.6 copy.15
  165.3 0.0 copy-done.1
  165.3 0.6 copy.16
  165.9 0.0 copy-done
  165.9 0.6 copy.17
  (4 shorter events, 0.1 us)
Async XLA Ops:
  0.6 7.2 %copy-start.4 = (s32[1,12]{1,0:T(1,128)S(1)}, s32[1,12]{1,0:T(1,128)}, u32[]{:S(2)}) copy-start(s32[1,12]{1,0:T(1,128)} %param.11) | copy-start | bytes 148
  41.6 42.6 %copy-start.3 = (s32[384]{0:T(512)}, s32[384]{0:T(512)S(1)}, u32[]{:S(2)}) copy-start(s32[384]{0:T(512)S(1)} %get-tuple-element.35.target) | copy-start | bytes 4612
  162.5 2.1 %copy-start.2 = (f32[32,256]{1,0:T(8,128)S(1)}, f32[32,256]{1,0:T(8,128)}, u32[]{:S(2)}) copy-start(f32[32,256]{1,0:T(8,128)} %get-tuple-element.41) | copy-start | bytes 98308
  162.5 2.7 %copy-start.1 = (f32[32,256]{1,0:T(8,128)S(1)}, f32[32,256]{1,0:T(8,128)}, u32[]{:S(2)}) copy-start(f32[32,256]{1,0:T(8,128)} %get-tuple-element.42) | copy-start | bytes 98308
  162.5 3.3 %copy-start = (f32[32,256]{1,0:T(8,128)S(1)}, f32[32,256]{1,0:T(8,128)}, u32[]{:S(2)}) copy-start(f32[32,256]{1,0:T(8,128)} %get-tuple-element.29) | copy-start | bytes 98308
